TPU v7x, 32 devices: a whole 2x2x4 slice. The times are simulated.
32 devices in a mesh: dp: 8 (over y, x, core), expert: 4 (over z).
Axes of the slice: x: 2, y: 2, z: 4, core: 2. Of those that a mesh axis runs over, the one named last changes fastest.
Arguments:
- tokens: bfloat16 [12288, 1024], P(('dp', 'expert')), may hold values from -6 to 6
- cotangent: bfloat16 [12288, 1024], P(('dp', 'expert')), may hold values from -6 to 6
- routes: int32 [12288, 8], P(('dp', 'expert')), may hold values from 0 to 15, all different within a row; in each aligned block of 384 rows (0 to 383, 384 to 767, ...) at most 256 rows name the same one
- cont_ids: int32 [32, 128], P(('dp', 'expert')), may hold values from 0 to 1, never falling along the last dimension, each value on 1 to 96 neighbouring positions
- norm_gains: float32 [1024, 2], replicated, may hold values from 0.5 to 1.5
- gains_moment: float32 [1024, 2], P(('dp', 'expert')), may hold values from -192 to 192
- gains_average: float32 [1024, 2], P(('dp', 'expert')), may hold values from 0.5 to 1.5
- heads_in: bfloat16 [1024, 2048], replicated, may hold values from -0.5 to 0.5
- heads_in_master: float32 [1024, 2048], P(('dp', 'expert')), may hold values from -0.625 to 0.625
- heads_in_moment: float32 [1024, 2048], P(('dp', 'expert')), may hold values from -128 to 128
- heads_in_average: float32 [1024, 2048], P(('dp', 'expert')), may hold values from -0.625 to 0.625
- heads_out: bfloat16 [1024, 1024], replicated, may hold values from -1.5 to 1.5
- heads_out_master: float32 [1024, 1024], P(('dp', 'expert')), may hold values from -0.1875 to 0.1875
- heads_out_moment: float32 [1024, 1024], P(('dp', 'expert')), may hold values from -32 to 32
- heads_out_average: float32 [1024, 1024], P(('dp', 'expert')), may hold values from -0.1875 to 0.1875
- router: bfloat16 [1024, 16], replicated, may hold values from -0.09375 to 0.09375
- router_master: float32 [1024, 16], P(('dp', 'expert')), may hold values from -2.5 to 2.5
- router_moment: float32 [1024, 16], P(('dp', 'expert')), may hold values from -128 to 128
- router_average: float32 [1024, 16], P(('dp', 'expert')), may hold values from -2.5 to 2.5
- expert_in: bfloat16 [16, 1024, 1024], P('expert'), may hold values from -0.1875 to 0.1875
- expert_in_master: float32 [16, 1024, 1024], P('expert', 'dp'), may hold values from -0.25 to 0.25
- expert_in_moment: float32 [16, 1024, 1024], P('expert', 'dp'), may hold values from -16 to 16
- expert_in_average: float32 [16, 1024, 1024], P('expert', 'dp'), may hold values from -0.25 to 0.25
- expert_out: bfloat16 [16, 1024, 512], P('expert'), may hold values from -1 to 1
- expert_out_master: float32 [16, 1024, 512], P('expert', 'dp'), may hold values from -0.0546875 to 0.0546875
- expert_out_moment: float32 [16, 1024, 512], P('expert', 'dp'), may hold values from -3.5 to 3.5
- expert_out_average: float32 [16, 1024, 512], P('expert', 'dp'), may hold values from -0.0546875 to 0.0546875
Outputs:
- output: bfloat16 [12288, 1024], P(('dp', 'expert'))
- token_grad: float32 [12288, 1024], P(('dp', 'expert'))
- gains_next: float32 [1024, 2], P(('dp', 'expert'))
- gains_moment_next: float32 [1024, 2], P(('dp', 'expert'))
- gains_average_next: float32 [1024, 2], P(('dp', 'expert'))
- heads_in_next: float32 [1024, 2048], P(('dp', 'expert'))
- heads_in_moment_next: float32 [1024, 2048], P(('dp', 'expert'))
- heads_in_average_next: float32 [1024, 2048], P(('dp', 'expert'))
- heads_out_next: float32 [1024, 1024], P(('dp', 'expert'))
- heads_out_moment_next: float32 [1024, 1024], P(('dp', 'expert'))
- heads_out_average_next: float32 [1024, 1024], P(('dp', 'expert'))
- router_next: float32 [1024, 16], P(('dp', 'expert'))
- router_moment_next: float32 [1024, 16], P(('dp', 'expert'))
- router_average_next: float32 [1024, 16], P(('dp', 'expert'))
- expert_in_next: float32 [16, 1024, 1024], P('expert', 'dp')
- expert_in_moment_next: float32 [16, 1024, 1024], P('expert', 'dp')
- expert_in_average_next: float32 [16, 1024, 1024], P('expert', 'dp')
- expert_out_next: float32 [16, 1024, 512], P('expert', 'dp')
- expert_out_moment_next: float32 [16, 1024, 512], P('expert', 'dp')
- expert_out_average_next: float32 [16, 1024, 512], P('expert', 'dp')
Inputs may be any that keep to these rules, and one draw needn't show every extreme that they name: `routes`: each row names 8 different experts. Among the tokens of one group no expert is named more than 256 times, a bound that some block reaches. `cont_ids`: in each row the numbers never fall; each of the 2 continuations has 1 to 96 tokens.
All inputs are finite; a program needn't handle non-finite values.
Results may differ from a plain program's by a relative error of at most 0.017.
Values may be sent and summed in bfloat16 or wider, within the bound.
A program may use at most 256 MiB of HBM per device.

v0:
```python
import jax
import jax.numpy as jnp
from jax import lax
from jax.sharding import PartitionSpec as P

HEADS = 16
KV_HEADS = 8
HEAD_DIM = 64


EPS = 1e-06
SCALE = 0.015625
THETA = 10000.0
MOMENTUM = 0.9
DECAY = 0.8
RATE = 0.001
HIGHEST = lax.Precision.HIGHEST


def layout(labels_row, prompt_len):
    places = jnp.arange(prompt_len + labels_row.shape[0], dtype=jnp.int32)
    earlier = jnp.sum((labels_row[None, :] < labels_row[:, None]).astype(jnp.int32), axis=1)
    offset = places[prompt_len:] - prompt_len - earlier
    positions = jnp.concatenate([places[:prompt_len], prompt_len + offset]).astype(jnp.float32)
    labels = jnp.concatenate([jnp.full((prompt_len,), -1, jnp.int32), labels_row])
    allowed = (places[None, :] <= places[:, None]) & (
        (places[None, :] < prompt_len) | (labels[None, :] == labels[:, None])
    )
    return (positions, allowed)


def rope_tables(positions):
    middle = HEAD_DIM // 2
    frequency = THETA ** (-2.0 * jnp.arange(middle, dtype=jnp.float32) / HEAD_DIM)
    angles = positions[:, None] * frequency[None, :]
    angles = jnp.concatenate([angles, angles], axis=1)
    return (jnp.cos(angles)[:, None, :], jnp.sin(angles)[:, None, :])


def rotate(values, cosine, sine_table):
    middle = values.shape[-1] // 2
    turned = jnp.concatenate([-values[..., middle:], values[..., :middle]], axis=-1)
    return values * cosine + turned * sine_table


def unrotate(gradient, cosine, sine_table):
    middle = gradient.shape[-1] // 2
    shifted = gradient * sine_table
    return gradient * cosine + jnp.concatenate(
        [shifted[..., middle:], -shifted[..., :middle]], axis=-1
    )


def masked_scores(queries, key_rows, allowed):
    products = (
        jnp.einsum("qkgd,pkd->kgqp", queries, key_rows, preferred_element_type=jnp.float32) * SCALE
    )
    return jnp.where(allowed[None, None], products, -1e30)


def rms_parts(values, gain):
    factor = lax.rsqrt(jnp.mean(values * values, axis=-1, keepdims=True) + EPS)
    return (values * factor * gain, factor)


def rms_back(incoming, values, factor, gain):
    normed = values * factor
    gain_grad = jnp.sum(incoming * normed, axis=0)
    weighted = incoming * gain
    input_grad = factor * (weighted - normed * jnp.mean(weighted * normed, axis=-1, keepdims=True))
    return (input_grad, gain_grad)


def bank_total(values, scales, bank_hot):
    partial_value = jnp.einsum(
        "tk,tkp,tkd->tpd", scales, bank_hot, values.astype(jnp.float32), precision=HIGHEST
    )
    return jnp.sum(partial_value.astype(jnp.bfloat16).astype(jnp.float32), axis=1)


def update(gradient, master, moment, average):
    moment_next = MOMENTUM * moment + gradient
    master_next = master - RATE * (gradient + MOMENTUM * moment_next)
    return (master_next, moment_next, DECAY * average + (1.0 - DECAY) * master_next)


def body(
    tokens,
    cotangent,
    routes,
    cont_ids,
    norm_gains,
    gains_moment,
    gains_average,
    heads_in,
    heads_in_master,
    heads_in_moment,
    heads_in_average,
    heads_out,
    heads_out_master,
    heads_out_moment,
    heads_out_average,
    router,
    router_master,
    router_moment,
    router_average,
    expert_in,
    expert_in_master,
    expert_in_moment,
    expert_in_average,
    expert_out,
    expert_out_master,
    expert_out_moment,
    expert_out_average,
):
    token_count, model_width = tokens.shape
    fanout = routes.shape[1]
    local_experts = expert_in.shape[0]
    peer_count = lax.axis_size("expert")
    experts = local_experts * peer_count
    capacity = 4 * token_count * fanout // (3 * experts)
    ff_width = expert_out.shape[2]
    group_size = HEADS // KV_HEADS
    query_end = HEADS * HEAD_DIM
    key_end = query_end + KV_HEADS * HEAD_DIM
    token_rows = tokens.astype(jnp.float32)
    normed_one, factor_one = rms_parts(token_rows, norm_gains[:, 0])
    first_in = normed_one.astype(jnp.bfloat16)
    projected = jnp.dot(first_in, heads_in, preferred_element_type=jnp.float32)
    positions, allowed = layout(cont_ids[0], token_count - cont_ids.shape[1])
    cosine, sine_table = rope_tables(positions)
    queries = rotate(
        projected[:, :query_end].reshape(token_count, HEADS, HEAD_DIM), cosine, sine_table
    )
    queries = queries.astype(jnp.bfloat16).reshape(token_count, KV_HEADS, group_size, HEAD_DIM)
    key_rows = rotate(
        projected[:, query_end:key_end].reshape(token_count, KV_HEADS, HEAD_DIM), cosine, sine_table
    ).astype(jnp.bfloat16)
    value_rows = (
        projected[:, key_end:].reshape(token_count, KV_HEADS, HEAD_DIM).astype(jnp.bfloat16)
    )
    scores = masked_scores(queries, key_rows, allowed)
    row_peak = jnp.max(scores, axis=-1, keepdims=True)
    log_total = row_peak + jnp.log(jnp.sum(jnp.exp(scores - row_peak), axis=-1, keepdims=True))
    weights = jnp.exp(scores - log_total).astype(jnp.bfloat16)
    attended = jnp.einsum("kgqp,pkd->qkgd", weights, value_rows, preferred_element_type=jnp.float32)
    attended = attended.reshape(token_count, query_end).astype(jnp.bfloat16)
    branch = jnp.einsum("th,dh->td", attended, heads_out, preferred_element_type=jnp.float32)
    hidden = token_rows + branch
    normed_two, factor_two = rms_parts(hidden, norm_gains[:, 1])
    second_in = normed_two.astype(jnp.bfloat16)
    logits = jnp.dot(second_in, router, preferred_element_type=jnp.float32)
    gate_probs = jax.nn.softmax(jnp.take_along_axis(logits, routes, axis=1), axis=-1)
    incoming = cotangent.astype(jnp.float32)
    matches = (routes[:, :, None] == jnp.arange(experts, dtype=jnp.int32)[None, None, :]).astype(
        jnp.int32
    )
    counts = jnp.sum(matches, axis=1)
    before = jnp.cumsum(counts, axis=0) - counts
    flat_rows = routes * capacity + jnp.take_along_axis(before, routes, axis=1)
    token_ids = jnp.broadcast_to(jnp.arange(token_count, dtype=jnp.int32)[:, None], routes.shape)
    slot_tokens = (
        jnp.full((experts * capacity,), token_count, jnp.int32)
        .at[flat_rows.reshape(-1)]
        .set(token_ids.reshape(-1))
    )
    slot_picks = (
        jnp.full((experts * capacity,), token_count * fanout, jnp.int32)
        .at[flat_rows.reshape(-1)]
        .set(jnp.arange(token_count * fanout, dtype=jnp.int32))
    )
    slot_gates = jnp.take(gate_probs.reshape(-1), slot_picks, axis=0, mode="fill", fill_value=0.0)
    peer_ids = jnp.arange(peer_count, dtype=jnp.int32)
    owners = routes // local_experts
    bank_hot = (owners[:, :, None] == peer_ids[None, None, :]).astype(jnp.float32)
    outgoing = jnp.take(second_in, slot_tokens, axis=0, mode="fill", fill_value=0).reshape(
        experts, capacity, model_width
    )
    inputs = lax.all_to_all(outgoing, "expert", split_axis=0, concat_axis=1, tiled=True)
    gate_up = jnp.einsum("erd,edf->erf", inputs, expert_in, preferred_element_type=jnp.float32)
    gate_part = gate_up[..., :ff_width]
    up_part = gate_up[..., ff_width:]
    activated = (jax.nn.silu(gate_part) * up_part).astype(jnp.bfloat16)
    result = jnp.einsum(
        "erf,edf->erd", activated, expert_out, preferred_element_type=jnp.float32
    ).astype(jnp.bfloat16)
    returned = lax.all_to_all(result, "expert", split_axis=1, concat_axis=0, tiled=True).reshape(
        experts * capacity, model_width
    )
    chosen = jnp.take(returned, flat_rows.reshape(-1), axis=0).reshape(
        token_count, fanout, model_width
    )
    mixture = bank_total(chosen, gate_probs, bank_hot)
    grad_gates = jnp.einsum("td,tkd->tk", cotangent, chosen, preferred_element_type=jnp.float32)
    outgoing_grads = (
        slot_gates[:, None] * jnp.take(cotangent, slot_tokens, axis=0, mode="fill", fill_value=0)
    ).astype(jnp.bfloat16)
    grad_result = lax.all_to_all(
        outgoing_grads.reshape(experts, capacity, model_width),
        "expert",
        split_axis=0,
        concat_axis=1,
        tiled=True,
    )
    output = (hidden + mixture).astype(jnp.bfloat16)
    grad_activated = jnp.einsum(
        "erd,edf->erf", grad_result, expert_out, preferred_element_type=jnp.float32
    )
    sigmoid_gate = jax.nn.sigmoid(gate_part)
    grad_gate_part = (
        grad_activated * up_part * sigmoid_gate * (1.0 + gate_part * (1.0 - sigmoid_gate))
    )
    grad_up_part = grad_activated * (gate_part * sigmoid_gate)
    grad_gate_up = jnp.concatenate([grad_gate_part, grad_up_part], axis=-1).astype(jnp.bfloat16)
    grad_expert_out = jnp.einsum(
        "erd,erf->edf", grad_result, activated, preferred_element_type=jnp.float32
    )
    grad_expert_in = jnp.einsum(
        "erd,erf->edf", inputs, grad_gate_up, preferred_element_type=jnp.float32
    )
    grad_inputs = jnp.einsum(
        "erf,edf->erd", grad_gate_up, expert_in, preferred_element_type=jnp.float32
    ).astype(jnp.bfloat16)
    returned_grads = lax.all_to_all(
        grad_inputs, "expert", split_axis=1, concat_axis=0, tiled=True
    ).reshape(experts * capacity, model_width)
    gathered_grads = jnp.take(returned_grads, flat_rows.reshape(-1), axis=0).reshape(
        token_count, fanout, model_width
    )
    grad_second = bank_total(gathered_grads, jnp.ones((token_count, fanout), jnp.float32), bank_hot)
    weighted_sum = jnp.sum(gate_probs * grad_gates, axis=1, keepdims=True)
    grad_picked = gate_probs * (grad_gates - weighted_sum)
    grad_logits = jnp.einsum(
        "tk,tke->te", grad_picked, matches.astype(jnp.float32), precision=HIGHEST
    )
    grad_router = jnp.dot(second_in.astype(jnp.float32).T, grad_logits, precision=HIGHEST)
    grad_second = grad_second + jnp.dot(
        grad_logits, router.astype(jnp.float32).T, precision=HIGHEST
    )
    grad_hidden_norm, grad_gain_two = rms_back(grad_second, hidden, factor_two, norm_gains[:, 1])
    grad_hidden = incoming + grad_hidden_norm
    grad_branch = grad_hidden.astype(jnp.bfloat16)
    grad_heads_out = jnp.einsum(
        "td,th->dh", grad_branch, attended, preferred_element_type=jnp.float32
    )
    grad_attended = jnp.dot(grad_branch, heads_out, preferred_element_type=jnp.float32).astype(
        jnp.bfloat16
    )
    grad_attended = grad_attended.reshape(token_count, KV_HEADS, group_size, HEAD_DIM)
    weight_full = jnp.exp(masked_scores(queries, key_rows, allowed) - log_total)
    grad_weights = jnp.einsum(
        "qkgd,pkd->kgqp", grad_attended, value_rows, preferred_element_type=jnp.float32
    )
    spread = jnp.sum(weight_full * grad_weights, axis=-1, keepdims=True)
    grad_scores = (weight_full * (grad_weights - spread)).astype(jnp.bfloat16)
    grad_queries = (
        jnp.einsum("kgqp,pkd->qkgd", grad_scores, key_rows, preferred_element_type=jnp.float32)
        * SCALE
    )
    grad_keys = (
        jnp.einsum("kgqp,qkgd->pkd", grad_scores, queries, preferred_element_type=jnp.float32)
        * SCALE
    )
    grad_values = jnp.einsum(
        "kgqp,qkgd->pkd",
        weight_full.astype(jnp.bfloat16),
        grad_attended,
        preferred_element_type=jnp.float32,
    )
    grad_projected = jnp.concatenate(
        [
            unrotate(
                grad_queries.reshape(token_count, HEADS, HEAD_DIM), cosine, sine_table
            ).reshape(token_count, query_end),
            unrotate(grad_keys, cosine, sine_table).reshape(token_count, KV_HEADS * HEAD_DIM),
            grad_values.reshape(token_count, KV_HEADS * HEAD_DIM),
        ],
        axis=1,
    ).astype(jnp.bfloat16)
    grad_heads_in = jnp.einsum(
        "td,tc->dc", first_in, grad_projected, preferred_element_type=jnp.float32
    )
    grad_first = jnp.einsum(
        "tc,dc->td", grad_projected, heads_in, preferred_element_type=jnp.float32
    )
    grad_tokens_norm, grad_gain_one = rms_back(grad_first, token_rows, factor_one, norm_gains[:, 0])
    token_grad = grad_hidden + grad_tokens_norm
    grad_gains = jnp.stack([grad_gain_one, grad_gain_two], axis=1)
    summed = (
        lax.psum_scatter(grad_heads_in, ("dp", "expert"), scatter_dimension=0, tiled=True),
        lax.psum_scatter(grad_heads_out, ("dp", "expert"), scatter_dimension=0, tiled=True),
        lax.psum_scatter(grad_router, ("dp", "expert"), scatter_dimension=0, tiled=True),
        lax.psum_scatter(grad_gains, ("dp", "expert"), scatter_dimension=0, tiled=True),
    )
    expert_sums = (
        lax.psum_scatter(
            grad_expert_in.astype(jnp.bfloat16), "dp", scatter_dimension=1, tiled=True
        ).astype(jnp.float32),
        lax.psum_scatter(
            grad_expert_out.astype(jnp.bfloat16), "dp", scatter_dimension=1, tiled=True
        ).astype(jnp.float32),
    )
    shard_rows = model_width // lax.axis_size(("dp", "expert"))
    gains_share = lax.dynamic_slice_in_dim(
        norm_gains, lax.axis_index(("dp", "expert")) * shard_rows, shard_rows, 0
    )
    gains_new = update(summed[3], gains_share, gains_moment, gains_average)
    inproj_new = update(summed[0], heads_in_master, heads_in_moment, heads_in_average)
    outproj_new = update(summed[1], heads_out_master, heads_out_moment, heads_out_average)
    router_new = update(summed[2], router_master, router_moment, router_average)
    upper_new = update(expert_sums[0], expert_in_master, expert_in_moment, expert_in_average)
    lower_new = update(expert_sums[1], expert_out_master, expert_out_moment, expert_out_average)
    return (
        output,
        token_grad,
        gains_new[0],
        gains_new[1],
        gains_new[2],
        inproj_new[0],
        inproj_new[1],
        inproj_new[2],
        outproj_new[0],
        outproj_new[1],
        outproj_new[2],
        router_new[0],
        router_new[1],
        router_new[2],
        upper_new[0],
        upper_new[1],
        upper_new[2],
        lower_new[0],
        lower_new[1],
        lower_new[2],
    )


def solution(mesh):
    return jax.shard_map(
        body,
        mesh=mesh,
        in_specs=(
            P(("dp", "expert"), None),
            P(("dp", "expert"), None),
            P(("dp", "expert"), None),
            P(("dp", "expert"), None),
            P(),
            P(("dp", "expert"), None),
            P(("dp", "expert"), None),
            P(),
            P(("dp", "expert"), None),
            P(("dp", "expert"), None),
            P(("dp", "expert"), None),
            P(),
            P(("dp", "expert"), None),
            P(("dp", "expert"), None),
            P(("dp", "expert"), None),
            P(),
            P(("dp", "expert"), None),
            P(("dp", "expert"), None),
            P(("dp", "expert"), None),
            P("expert", None, None),
            P("expert", "dp", None),
            P("expert", "dp", None),
            P("expert", "dp", None),
            P("expert", None, None),
            P("expert", "dp", None),
            P("expert", "dp", None),
            P("expert", "dp", None),
        ),
        out_specs=(
            P(("dp", "expert"), None),
            P(("dp", "expert"), None),
            P(("dp", "expert"), None),
            P(("dp", "expert"), None),
            P(("dp", "expert"), None),
            P(("dp", "expert"), None),
            P(("dp", "expert"), None),
            P(("dp", "expert"), None),
            P(("dp", "expert"), None),
            P(("dp", "expert"), None),
            P(("dp", "expert"), None),
            P(("dp", "expert"), None),
            P(("dp", "expert"), None),
            P(("dp", "expert"), None),
            P("expert", "dp", None),
            P("expert", "dp", None),
            P("expert", "dp", None),
            P("expert", "dp", None),
            P("expert", "dp", None),
            P("expert", "dp", None),
        ),
        check_vma=False,
    )
```

profile of v0, /device:TPU:0, one launch (start us, length us, event | category | flops | bytes accessed | tf_op | source)
XLA Modules:
  0.0 1631.6 jit_solution(6618232595936007298)
XLA Ops:
  9.5 4.3 fusion.56
  17.6 3.0 copy.184
  20.6 2.6 slice_negate_fusion.1
  24.4 1.5 copy.183
  29.9 2.3 fusion.33
  32.3 1.6 fusion.13
  33.9 1.9 exponential_reduce_fusion
  35.8 1.7 copy-done.2
  37.5 2.4 convolution_convert_fusion.5
  39.9 2.2 multiply_reduce_fusion.2
  42.7 1.6 multiply_convert_fusion.4
  44.7 25.2 %gather_fusion.1 = f32[3072]{0:T(1024)S(1)} fusion(f32[384,16]{0,1:T(8,128)S(1)} %fusion.96, s32[3072]{0:T(1024)S(1)} %reshape.416), kind=kCustom, calls=%fused_computation.5 | custom fusion | bytes 49152 | tf_op jit(solution)/shard_map/jit(take_along_axis)/gather | solution.py:153
  72.1 20.2 %gather_fusion.2 = s32[3072]{0:T(1024)S(1)} fusion(s32[384,16]{1,0:T(8,128)S(1)} %bitcast_subtract_fusion.1, s32[3072]{0:T(1024)S(1)} %reshape.416), kind=kCustom, calls=%fused_computation.6 | custom fusion | bytes 49152 | tf_op jit(solution)/shard_map/jit(take_along_axis)/gather | solution.py:160
  93.5 11.8 scatter_custom_fusion
  105.4 18.3 %gather_fusion.3 = bf16[4096,1024]{1,0:T(8,128)(2,1)} fusion(bf16[384,1024]{1,0:T(8,128)(2,1)S(1)} %multiply_convert_fusion.4, s32[4096]{0:T(1024)S(1)} %fusion.65), kind=kCustom, calls=%fused_computation.clone | custom fusion | bytes 16793600 | tf_op jit(solution)/shard_map/jit(_take)/gather | solution.py:176
  123.7 4.4 broadcast_select_fusion
  128.1 189.2 %all_to_all.66 = bf16[16,256,1024]{2,1,0:T(8,128)(2,1)} all-to-all(bf16[16,256,1024]{2,1,0:T(8,128)(2,1)S(1)} %bitcast.173), channel_id=1, replica_groups=mesh['dp'=8,'expert'=4] {'expert'}, dimensions={0} | all-to-all | bytes 16777216 | tf_op jit(solution)/shard_map/all_to_all | solution.py:179
  317.3 8.0 copy.198
  325.3 17.0 %fusion.97 = f32[4,1024,1024]{1,2,0:T(8,128)} fusion(bf16[4,1024,1024]{2,1,0:T(8,128)(2,1)} %bitcast.178, bf16[4,1024,1024]{2,1,0:T(8,128)(2,1)} %param.50), kind=kOutput, calls=%fused_computation.204 | convolution fusion | flops 8589934592 | bytes 33554432 | tf_op jit(solution)/shard_map/erd,edf->erf/dot_general | solution.py:180
  342.3 8.5 multiply_convert_fusion.3
  350.9 11.6 convolution_convert_fusion.2
  362.5 22.5 %copy.201 = bf16[4,1024,1024]{2,0,1:T(4,128)(2,1)} copy(bf16[4,1024,1024]{2,1,0:T(8,128)(2,1)} %convolution_convert_fusion.2) | data formatting | bytes 16777216 | tf_op jit(solution)/shard_map/convert_element_type | solution.py:186
  385.0 5.6 all-to-all-start.1
  390.8 22.1 %gather_fusion.5 = bf16[4096,1024]{1,0:T(8,128)(2,1)} fusion(bf16[384,1024]{1,0:T(8,128)(2,1)} %param.32, s32[4096]{0:T(1024)S(1)} %fusion.65), kind=kCustom, calls=%fused_computation.2.clone | custom fusion | bytes 16793600 | tf_op jit(solution)/shard_map/jit(_take)/gather | solution.py:196
  412.9 11.8 scatter_custom_fusion.1
  424.8 148.0 %all-to-all-done.1 = bf16[4,1024,1024]{2,0,1:T(4,128)(2,1)} async-done(((bf16[4,1024,1024]{2,0,1:T(4,128)(2,1)}), bf16[4,1024,1024]{2,0,1:T(4,128)(2,1)}, u32[]{:S(2)}, u32[]{:S(2)}) %all-to-all-start.1) | async-done | bytes 8388640 | tf_op jit(solution)/shard_map/all_to_all | solution.py:187
  572.8 9.8 copy.202
  582.6 20.4 %gather_fusion.4 = bf16[3072,1024]{1,0:T(8,128)(2,1)} fusion(bf16[4096,1024]{1,0:T(8,128)(2,1)} %bitcast.168, s32[3072]{0:T(1024)S(1)} %fusion.72), kind=kCustom, calls=%fused_computation.1.clone | custom fusion | bytes 12595200 | tf_op jit(solution)/shard_map/jit(_take)/gather | solution.py:190
  603.0 7.6 fusion.7
  611.0 23.0 %gather_fusion = f32[4096]{0:T(1024)S(1)} fusion(f32[3072]{0:T(1024)S(1)} %div.58, s32[4096]{0:T(1024)S(1)} %fusion.64), kind=kCustom, calls=%fused_computation.4 | custom fusion | bytes 49152 | tf_op jit(solution)/shard_map/jit(_take)/gather | solution.py:172
  634.1 7.8 multiply_convert_fusion
  641.9 5.6 all-to-all-start.2
  647.6 1.7 fusion.98
  649.3 186.8 %all-to-all-done.2 = bf16[16,256,1024]{2,1,0:T(8,128)(2,1)} async-done(((bf16[16,256,1024]{2,1,0:T(8,128)(2,1)}), bf16[16,256,1024]{2,1,0:T(8,128)(2,1)}, u32[]{:S(2)}, u32[]{:S(2)}) %all-to-all-start.2) | async-done | bytes 8388640 | tf_op jit(solution)/shard_map/all_to_all | solution.py:198
  836.1 8.1 copy.204
  844.2 15.5 multiply_convert_fusion.2
  859.7 16.5 %convolution_convert_fusion.1 = bf16[4,1024,1024]{2,1,0:T(8,128)(2,1)} fusion(bf16[4,1024,1024]{2,1,0:T(8,128)(2,1)} %param.50, bf16[4,1024,512]{1,2,0:T(8,128)(2,1)} %get-tuple-element.49, bf16[4,1024,512]{1,2,0:T(8,128)(2,1)} %get-tuple-element.48), kind=kOutput, calls=%fused_computation.27 | convolution fusion | flops 8610906112 | bytes 25165824 | tf_op jit(solution)/shard_map/erf,edf->erd/dot_general | solution.py:221
  876.1 12.1 copy.207
  888.3 5.6 all-to-all-start.3
  894.4 11.8 convolution_convert_fusion.3
  906.2 16.3 %convolution_convert_fusion = bf16[4,1024,1024]{2,1,0:T(8,128)(2,1)} fusion(bf16[4,1024,1024]{2,1,0:T(8,128)(2,1)} %bitcast.179, bf16[4,1024,512]{1,2,0:T(8,128)(2,1)} %get-tuple-element.49, bf16[4,1024,512]{1,2,0:T(8,128)(2,1)} %get-tuple-element.48), kind=kOutput, calls=%fused_computation.26 | convolution fusion | flops 8610906112 | bytes 25165824 | tf_op jit(solution)/shard_map/erd,erf->edf/dot_general | solution.py:218
  923.4 11.6 convert_reduce_fusion.1
  935.0 141.3 %all-to-all-done.3 = bf16[4,1024,1024]{2,0,1:T(4,128)(2,1)} async-done(((bf16[4,1024,1024]{2,0,1:T(4,128)(2,1)}), bf16[4,1024,1024]{2,0,1:T(4,128)(2,1)}, u32[]{:S(2)}, u32[]{:S(2)}) %all-to-all-start.3) | async-done | bytes 8388640 | tf_op jit(solution)/shard_map/all_to_all | solution.py:224
  1076.3 9.7 copy.208
  1086.1 20.4 %gather_fusion.6 = bf16[3072,1024]{1,0:T(8,128)(2,1)} fusion(bf16[4096,1024]{1,0:T(8,128)(2,1)} %bitcast.167, s32[3072]{0:T(1024)S(1)} %fusion.72), kind=kCustom, calls=%fused_computation.3.clone | custom fusion | bytes 12595200 | tf_op jit(solution)/shard_map/jit(_take)/gather | solution.py:227
  1106.5 7.2 convert_reduce_fusion
  1117.9 1.9 convolution_convert_fusion.4
  1119.8 1.5 copy.209
  1121.3 7.9 fusion
  1129.2 11.4 fusion.2
  1140.7 3.4 convolution_multiply_fusion
  1145.8 1.5 broadcast_multiply_fusion
  1149.0 2.4 fusion.37
  1151.4 3.2 fusion.30
  1155.8 4.9 fusion.48
  1161.1 7.1 fusion.44
  1169.7 4.2 multiply_add_fusion.2
  1173.9 1.6 fusion.29
  1175.6 7.1 multiply_add_fusion
  1182.8 106.7 %reduce-scatter.19.cloned.1.call-done = f32[32,2]{1,0:T(8,128)} async-done(((f32[1024,2]{1,0:T(8,128)}), f32[32,2]{1,0:T(8,128)}) %reduce-scatter.19.cloned.1.call-update) | async-done | bytes 272
  1291.6 144.2 %reduce-scatter.13.cloned.1.call-done = f32[32,1024]{1,0:T(8,128)} async-done(((f32[1024,1024]{1,0:T(8,128)}), f32[32,1024]{1,0:T(8,128)}) %reduce-scatter.13.cloned.1.call-update) | async-done | bytes 131088 | tf_op jit(solution)/shard_map/reduce_scatter | solution.py:291
  1435.8 1.7 multiply_add_fusion.5
  1437.5 184.9 %reduce-scatter.11.cloned.1.call-done = f32[32,2048]{1,0:T(8,128)} async-done(((f32[1024,2048]{1,0:T(8,128)}), f32[32,2048]{1,0:T(8,128)}) %reduce-scatter.11.cloned.1.call-update) | async-done | bytes 262160 | tf_op jit(solution)/shard_map/reduce_scatter | solution.py:290
  1622.4 1.9 multiply_add_fusion.3
  (227 shorter events, 29.9 us)
Async XLA Ops:
  7.2 32.7 %copy-start = (bf16[1024,1024]{1,0:T(8,128)(2,1)S(1)}, bf16[1024,1024]{1,0:T(8,128)(2,1)}, u32[]{:S(2)}) copy-start(bf16[1024,1024]{1,0:T(8,128)(2,1)} %param.42) | copy-start | bytes 6291460
  8.1 5.7 copy-start.34
  8.1 34.3 %copy-start.46 = (f32[1024,1]{0,1:T(1,128)}, f32[1024,1]{0,1:T(1,128)S(1)}, u32[]{:S(2)}) copy-start(f32[1024,1]{0,1:T(1,128)S(1)} %get-tuple-element.66) | copy-start | bytes 12292
  9.5 4.3 copy-start.48
  13.8 2.3 copy-start.30
  15.1 8.1 copy-start.59
  24.4 7.8 copy-start.17
  24.4 7.8 copy-start.21
  28.6 7.2 copy-start.12
  29.9 3.9 copy-start.10
  32.2 1.6 copy-start.8
  33.8 3.7 copy-start.2
  33.9 3.6 copy-start.23
  35.8 4.1 copy-start.36
  37.5 2.4 copy-start.6
  39.9 2.2 copy-start.26
  39.9 4.4 copy-start.40
  44.6 26.0 %copy-start.45 = (s32[16,3,128]{2,0,1:T(8,128)S(1)}, s32[16,3,128]{2,0,1:T(8,128)}, u32[]{:S(2)}) copy-start(s32[16,3,128]{2,0,1:T(8,128)} %copy_bitcast_fusion) | copy-start | bytes 73732
  44.6 27.4 %copy-start.25 = (s32[384,16]{1,0:T(8,128)S(1)}, s32[384,16]{1,0:T(8,128)}, u32[]{:S(2)}) copy-start(s32[384,16]{1,0:T(8,128)} %copy.194) | copy-start | bytes 73732
  70.1 1.8 copy-start.38
  385.0 187.8 %all-to-all-start.1 = ((bf16[4,1024,1024]{2,0,1:T(4,128)(2,1)}), bf16[4,1024,1024]{2,0,1:T(4,128)(2,1)}, u32[]{:S(2)}, u32[]{:S(2)}) async-start(bf16[4,1024,1024]{2,0,1:T(4,128)(2,1)} %copy.201), calls=%async_computation.1 | async-start | bytes 16777216 | tf_op jit(solution)/shard_map/all_to_all | solution.py:187
  390.7 34.0 %copy-start.39 = (f32[384,8]{0,1:T(8,128)S(1)}, f32[384,8]{0,1:T(8,128)}, u32[]{:S(2)}) copy-start(f32[384,8]{0,1:T(8,128)} %copy-done.38) | copy-start | bytes 36868
  390.8 34.0 %copy-start.53 = (f32[384]{0:T(512)S(1)}, f32[384]{0:T(512)}, u32[]{:S(2)}) copy-start(f32[384]{0:T(512)} %get-tuple-element.46) | copy-start | bytes 4612
  641.9 194.2 %all-to-all-start.2 = ((bf16[16,256,1024]{2,1,0:T(8,128)(2,1)}), bf16[16,256,1024]{2,1,0:T(8,128)(2,1)}, u32[]{:S(2)}, u32[]{:S(2)}) async-start(bf16[16,256,1024]{2,1,0:T(8,128)(2,1)} %bitcast.174), calls=%async_computation.2 | async-start | bytes 16777216 | tf_op jit(solution)/shard_map/all_to_all | solution.py:198
  647.5 520.8 %reduce-scatter.21.cloned.1.call-start = ((), (), s32[]{:S(2)}) async-start(), calls=%async_computation.15 | async-start | bytes 540672
  888.3 188.1 %all-to-all-start.3 = ((bf16[4,1024,1024]{2,0,1:T(4,128)(2,1)}), bf16[4,1024,1024]{2,0,1:T(4,128)(2,1)}, u32[]{:S(2)}, u32[]{:S(2)}) async-start(bf16[4,1024,1024]{2,0,1:T(4,128)(2,1)} %copy.207), calls=%async_computation.3 | async-start | bytes 16777216 | tf_op jit(solution)/shard_map/all_to_all | solution.py:224
  893.9 275.8 %reduce-scatter.17.cloned.1.call-start = ((), (), s32[]{:S(2)}) async-start(), calls=%async_computation.13 | async-start | bytes 4718592 | tf_op jit(solution)/shard_map/reduce_scatter | solution.py:299
  906.2 269.4 %reduce-scatter.15.cloned.1.call-start = ((), (), s32[]{:S(2)}) async-start(), calls=%async_computation.12 | async-start | bytes 9437184 | tf_op jit(solution)/shard_map/reduce_scatter | solution.py:296
  922.6 366.9 %reduce-scatter.19.cloned.1.call-start = ((), (), s32[]{:S(2)}) async-start(), calls=%async_computation.14 | async-start | bytes 540672
  1106.5 7.3 copy-start.5
  1106.5 7.3 copy-start.41
  1106.5 7.3 copy-start.47
  1106.5 7.3 copy-start.52
  1113.8 1.6 copy-start.20
  1117.9 3.4 copy-start.13
  1117.9 3.4 copy-start.24
  1117.9 3.4 copy-start.37
  1121.3 7.9 copy-start.14
  1129.2 11.4 copy-start.11
  1140.7 3.5 copy-start.18
  1140.7 4.6 slice-start.3
  1144.2 3.4 slice-start
  1144.5 3.9 slice-start.1
  1145.2 6.1 copy-start.16
  1145.8 1.7 copy-start.28
  1145.8 2.9 slice-start.2
  1145.8 3.1 copy-start.15
  1149.0 2.4 copy-start.7
  1149.0 2.4 copy-start.35
  1149.0 2.5 copy-start.49
  1149.0 2.5 copy-start.60
  1151.4 3.3 copy-start.29
  1155.7 280.0 %reduce-scatter.13.cloned.1.call-start = ((), (), s32[]{:S(2)}) async-start(), calls=%async_computation.11 | async-start | bytes 4325376 | tf_op jit(solution)/shard_map/reduce_scatter | solution.py:291
  1160.7 461.6 %reduce-scatter.11.cloned.1.call-start = ((), (), s32[]{:S(2)}) async-start(), calls=%async_computation.10 | async-start | bytes 8650752 | tf_op jit(solution)/shard_map/reduce_scatter | solution.py:290
  1169.7 4.2 copy-start.4
  1169.7 4.2 copy-start.19
  1175.5 114.7 %copy-start.57 = (f32[32,2]{0,1:T(2,128)S(1)}, f32[32,2]{0,1:T(2,128)}, u32[]{:S(2)}) copy-start(f32[32,2]{0,1:T(2,128)} %param.37) | copy-start | bytes 772
  1175.5 114.7 %copy-start.58 = (f32[32,2]{0,1:T(2,128)S(1)}, f32[32,2]{0,1:T(2,128)}, u32[]{:S(2)}) copy-start(f32[32,2]{0,1:T(2,128)} %param.36) | copy-start | bytes 772
  1175.5 260.2 %copy-start.42 = (f32[32,1024]{1,0:T(8,128)S(1)}, f32[32,1024]{1,0:T(8,128)}, u32[]{:S(2)}) copy-start(f32[32,1024]{1,0:T(8,128)} %param.45) | copy-start | bytes 393220
  1175.5 260.2 %copy-start.43 = (f32[32,1024]{1,0:T(8,128)S(1)}, f32[32,1024]{1,0:T(8,128)}, u32[]{:S(2)}) copy-start(f32[32,1024]{1,0:T(8,128)} %param.43) | copy-start | bytes 393220
  1175.5 260.2 %copy-start.44 = (f32[32,1024]{1,0:T(8,128)S(1)}, f32[32,1024]{1,0:T(8,128)}, u32[]{:S(2)}) copy-start(f32[32,1024]{1,0:T(8,128)} %param.44) | copy-start | bytes 393220
  1175.6 446.8 %copy-start.31 = (f32[32,2048]{1,0:T(8,128)S(1)}, f32[32,2048]{1,0:T(8,128)}, u32[]{:S(2)}) copy-start(f32[32,2048]{1,0:T(8,128)} %param.41) | copy-start | bytes 786436
  1175.6 446.8 %copy-start.32 = (f32[32,2048]{1,0:T(8,128)S(1)}, f32[32,2048]{1,0:T(8,128)}, u32[]{:S(2)}) copy-start(f32[32,2048]{1,0:T(8,128)} %param.39) | copy-start | bytes 786436
  1175.6 446.8 %copy-start.33 = (f32[32,2048]{1,0:T(8,128)S(1)}, f32[32,2048]{1,0:T(8,128)}, u32[]{:S(2)}) copy-start(f32[32,2048]{1,0:T(8,128)} %param.40) | copy-start | bytes 786436
  (11 other events, 10.9 us)
Sparse Core Ops, SparseCore 0:
  651.1 243.6 reduce-scatter.20
  906.3 52.8 reduce-scatter.16
  962.6 71.2 reduce-scatter.14
  1155.9 133.5 reduce-scatter.18
  1291.6 144.1 reduce-scatter.12
  1437.9 184.4 reduce-scatter.10
where the time goes:
time: 1640 us; the launch traced here: 1630 us
  waiting for transfers between devices  912 us (56%)
  local copies, waits for them, and re-layouts  267 us (16%)
  blocking collectives  189 us (12%)
  matrix products  161 us (10%)
  other arithmetic  68.7 us (4%)
  starting transfers between devices  17.9 us (1%)
    all_to_all x1, blocking collectives, body(): lax.all_to_all(outgoing, 'expert', split_axis=0, concat_axis=1, tiled=True)  189 us
    all_to_all x1, waiting for transfers between devices, body(): lax.all_to_all(outgoing_grads.reshape(experts, capacity, model_width), 'e...  187 us
    reduce_scatter x1, waiting for transfers between devices, body(): lax.psum_scatter(grad_heads_in, ('dp', 'expert'), scatter_dimension=0, ti...  185 us
    all_to_all x1, waiting for transfers between devices, body(): lax.all_to_all(result, 'expert', split_axis=1, concat_axis=0, tiled=True)  148 us
    reduce_scatter x1, waiting for transfers between devices, body(): lax.psum_scatter(grad_heads_out, ('dp', 'expert'), scatter_dimension=0, t...  144 us
    all_to_all x1, waiting for transfers between devices, body(): lax.all_to_all(grad_inputs, 'expert', split_axis=1, concat_axis=0, tiled=...  141 us
    unnamed x8, waiting for transfers between devices  107 us
  transfers between devices with their start and end apart: 9, of which 6 were waited for; matrix products, arithmetic and copies ran while one was open for 14% of the time, Pallas kernels for 0%

commit v1 on v0

--- a/solution.py
+++ b/solution.py
@@ -69,13 +69,6 @@
     weighted = incoming * gain
     input_grad = factor * (weighted - normed * jnp.mean(weighted * normed, axis=-1, keepdims=True))
     return (input_grad, gain_grad)
-
-
-def bank_total(values, scales, bank_hot):
-    partial_value = jnp.einsum(
-        "tk,tkp,tkd->tpd", scales, bank_hot, values.astype(jnp.float32), precision=HIGHEST
-    )
-    return jnp.sum(partial_value.astype(jnp.bfloat16).astype(jnp.float32), axis=1)
 
 
 def update(gradient, master, moment, average):
@@ -114,11 +107,9 @@
     expert_out_average,
 ):
     token_count, model_width = tokens.shape
-    fanout = routes.shape[1]
     local_experts = expert_in.shape[0]
     peer_count = lax.axis_size("expert")
     experts = local_experts * peer_count
-    capacity = 4 * token_count * fanout // (3 * experts)
     ff_width = expert_out.shape[2]
     group_size = HEADS // KV_HEADS
     query_end = HEADS * HEAD_DIM
@@ -150,89 +141,55 @@
     normed_two, factor_two = rms_parts(hidden, norm_gains[:, 1])
     second_in = normed_two.astype(jnp.bfloat16)
     logits = jnp.dot(second_in, router, preferred_element_type=jnp.float32)
-    gate_probs = jax.nn.softmax(jnp.take_along_axis(logits, routes, axis=1), axis=-1)
+    named = jnp.any(
+        routes[:, :, None] == jnp.arange(experts, dtype=jnp.int32)[None, None, :], axis=1
+    )
+    peak = jnp.max(jnp.where(named, logits, -jnp.inf), axis=1, keepdims=True)
+    powers = jnp.where(named, jnp.exp(logits - peak), 0.0)
+    gates = powers / jnp.sum(powers, axis=1, keepdims=True)
     incoming = cotangent.astype(jnp.float32)
-    matches = (routes[:, :, None] == jnp.arange(experts, dtype=jnp.int32)[None, None, :]).astype(
-        jnp.int32
-    )
-    counts = jnp.sum(matches, axis=1)
-    before = jnp.cumsum(counts, axis=0) - counts
-    flat_rows = routes * capacity + jnp.take_along_axis(before, routes, axis=1)
-    token_ids = jnp.broadcast_to(jnp.arange(token_count, dtype=jnp.int32)[:, None], routes.shape)
-    slot_tokens = (
-        jnp.full((experts * capacity,), token_count, jnp.int32)
-        .at[flat_rows.reshape(-1)]
-        .set(token_ids.reshape(-1))
-    )
-    slot_picks = (
-        jnp.full((experts * capacity,), token_count * fanout, jnp.int32)
-        .at[flat_rows.reshape(-1)]
-        .set(jnp.arange(token_count * fanout, dtype=jnp.int32))
-    )
-    slot_gates = jnp.take(gate_probs.reshape(-1), slot_picks, axis=0, mode="fill", fill_value=0.0)
-    peer_ids = jnp.arange(peer_count, dtype=jnp.int32)
-    owners = routes // local_experts
-    bank_hot = (owners[:, :, None] == peer_ids[None, None, :]).astype(jnp.float32)
-    outgoing = jnp.take(second_in, slot_tokens, axis=0, mode="fill", fill_value=0).reshape(
-        experts, capacity, model_width
-    )
-    inputs = lax.all_to_all(outgoing, "expert", split_axis=0, concat_axis=1, tiled=True)
-    gate_up = jnp.einsum("erd,edf->erf", inputs, expert_in, preferred_element_type=jnp.float32)
+    slots = lax.axis_index("expert") * local_experts
+    rows_all = lax.all_gather(second_in, "expert", axis=0, tiled=True)
+    cots_all = lax.all_gather(cotangent, "expert", axis=0, tiled=True)
+    gates_all = lax.all_gather(gates, "expert", axis=0, tiled=True)
+    gates_here = lax.dynamic_slice_in_dim(gates_all, slots, local_experts, 1)
+    gate_col = gates_here.T[:, :, None]
+    gate_up = jnp.einsum("td,edf->etf", rows_all, expert_in, preferred_element_type=jnp.float32)
     gate_part = gate_up[..., :ff_width]
     up_part = gate_up[..., ff_width:]
-    activated = (jax.nn.silu(gate_part) * up_part).astype(jnp.bfloat16)
-    result = jnp.einsum(
-        "erf,edf->erd", activated, expert_out, preferred_element_type=jnp.float32
-    ).astype(jnp.bfloat16)
-    returned = lax.all_to_all(result, "expert", split_axis=1, concat_axis=0, tiled=True).reshape(
-        experts * capacity, model_width
-    )
-    chosen = jnp.take(returned, flat_rows.reshape(-1), axis=0).reshape(
-        token_count, fanout, model_width
-    )
-    mixture = bank_total(chosen, gate_probs, bank_hot)
-    grad_gates = jnp.einsum("td,tkd->tk", cotangent, chosen, preferred_element_type=jnp.float32)
-    outgoing_grads = (
-        slot_gates[:, None] * jnp.take(cotangent, slot_tokens, axis=0, mode="fill", fill_value=0)
-    ).astype(jnp.bfloat16)
-    grad_result = lax.all_to_all(
-        outgoing_grads.reshape(experts, capacity, model_width),
+    sigmoid_gate = jax.nn.sigmoid(gate_part)
+    silu_gate = gate_part * sigmoid_gate
+    active = silu_gate * up_part
+    gated = (active * gate_col).astype(jnp.bfloat16)
+    mix_part = jnp.einsum("etf,edf->td", gated, expert_out, preferred_element_type=jnp.float32)
+    back = jnp.einsum("td,edf->etf", cots_all, expert_out, preferred_element_type=jnp.float32)
+    gate_grads_here = jnp.sum(active * back, axis=-1).T
+    grad_activated = back * gate_col
+    grad_gate_part = (
+        grad_activated * up_part * sigmoid_gate * (1.0 + gate_part * (1.0 - sigmoid_gate))
+    )
+    grad_up_part = grad_activated * silu_gate
+    grad_gate_up = jnp.concatenate([grad_gate_part, grad_up_part], axis=-1).astype(jnp.bfloat16)
+    grad_part = jnp.einsum("etf,edf->td", grad_gate_up, expert_in, preferred_element_type=jnp.float32)
+    grad_second = lax.psum_scatter(
+        grad_part.astype(jnp.bfloat16), "expert", scatter_dimension=0, tiled=True
+    ).astype(jnp.float32)
+    mixture = lax.psum_scatter(
+        mix_part.astype(jnp.bfloat16), "expert", scatter_dimension=0, tiled=True
+    ).astype(jnp.float32)
+    grad_expert_out = jnp.einsum("td,etf->edf", cots_all, gated, preferred_element_type=jnp.float32)
+    grad_expert_in = jnp.einsum(
+        "td,etf->edf", rows_all, grad_gate_up, preferred_element_type=jnp.float32
+    )
+    output = (hidden + mixture).astype(jnp.bfloat16)
+    grad_gates = lax.all_to_all(
+        gate_grads_here.reshape(peer_count, token_count, local_experts),
         "expert",
         split_axis=0,
-        concat_axis=1,
-        tiled=True,
-    )
-    output = (hidden + mixture).astype(jnp.bfloat16)
-    grad_activated = jnp.einsum(
-        "erd,edf->erf", grad_result, expert_out, preferred_element_type=jnp.float32
-    )
-    sigmoid_gate = jax.nn.sigmoid(gate_part)
-    grad_gate_part = (
-        grad_activated * up_part * sigmoid_gate * (1.0 + gate_part * (1.0 - sigmoid_gate))
-    )
-    grad_up_part = grad_activated * (gate_part * sigmoid_gate)
-    grad_gate_up = jnp.concatenate([grad_gate_part, grad_up_part], axis=-1).astype(jnp.bfloat16)
-    grad_expert_out = jnp.einsum(
-        "erd,erf->edf", grad_result, activated, preferred_element_type=jnp.float32
-    )
-    grad_expert_in = jnp.einsum(
-        "erd,erf->edf", inputs, grad_gate_up, preferred_element_type=jnp.float32
-    )
-    grad_inputs = jnp.einsum(
-        "erf,edf->erd", grad_gate_up, expert_in, preferred_element_type=jnp.float32
-    ).astype(jnp.bfloat16)
-    returned_grads = lax.all_to_all(
-        grad_inputs, "expert", split_axis=1, concat_axis=0, tiled=True
-    ).reshape(experts * capacity, model_width)
-    gathered_grads = jnp.take(returned_grads, flat_rows.reshape(-1), axis=0).reshape(
-        token_count, fanout, model_width
-    )
-    grad_second = bank_total(gathered_grads, jnp.ones((token_count, fanout), jnp.float32), bank_hot)
-    weighted_sum = jnp.sum(gate_probs * grad_gates, axis=1, keepdims=True)
-    grad_picked = gate_probs * (grad_gates - weighted_sum)
-    grad_logits = jnp.einsum(
-        "tk,tke->te", grad_picked, matches.astype(jnp.float32), precision=HIGHEST
-    )
+        concat_axis=0,
+    )
+    grad_gates = jnp.transpose(grad_gates, (1, 0, 2)).reshape(token_count, experts)
+    grad_logits = gates * (grad_gates - jnp.sum(gates * grad_gates, axis=1, keepdims=True))
     grad_router = jnp.dot(second_in.astype(jnp.float32).T, grad_logits, precision=HIGHEST)
     grad_second = grad_second + jnp.dot(
         grad_logits, router.astype(jnp.float32).T, precision=HIGHEST
@@ -285,12 +242,26 @@
     )
     grad_tokens_norm, grad_gain_one = rms_back(grad_first, token_rows, factor_one, norm_gains[:, 0])
     token_grad = grad_hidden + grad_tokens_norm
-    grad_gains = jnp.stack([grad_gain_one, grad_gain_two], axis=1)
+    head_grads = jnp.concatenate(
+        [
+            grad_heads_in,
+            grad_heads_out,
+            grad_router,
+            grad_gain_one[:, None],
+            grad_gain_two[:, None],
+        ],
+        axis=1,
+    ).astype(jnp.bfloat16)
+    head_sums = lax.psum_scatter(
+        head_grads, ("dp", "expert"), scatter_dimension=0, tiled=True
+    ).astype(jnp.float32)
+    cut_in = grad_heads_in.shape[1]
+    cut_out = cut_in + grad_heads_out.shape[1]
     summed = (
-        lax.psum_scatter(grad_heads_in, ("dp", "expert"), scatter_dimension=0, tiled=True),
-        lax.psum_scatter(grad_heads_out, ("dp", "expert"), scatter_dimension=0, tiled=True),
-        lax.psum_scatter(grad_router, ("dp", "expert"), scatter_dimension=0, tiled=True),
-        lax.psum_scatter(grad_gains, ("dp", "expert"), scatter_dimension=0, tiled=True),
+        head_sums[:, :cut_in],
+        head_sums[:, cut_in:cut_out],
+        head_sums[:, cut_out : cut_out + experts],
+        head_sums[:, cut_out + experts :],
     )
     expert_sums = (
         lax.psum_scatter(

time: 1640 us -> 713 us (0.43)
  waiting for transfers between devices: 912 us -> 310 us
  blocking collectives: 189 us -> 24.1 us
  local copies, waits for them, and re-layouts: 267 us -> 136 us
  matrix products: 161 us -> 144 us
    all_to_all x3 -> x1, waiting for transfers between devices: 476 us -> 5.52 us  [body(): lax.all_to_all(gate_grads_here.reshape(peer_count, token_count, local_exp...]
    reduce_scatter x4 -> x2, waiting for transfers between devices: 329 us -> 31.7 us  [the longest x1 31.7 us: body(): lax.psum_scatter(mix_part.astype(jnp.bfloat16), 'expert', scatter_dimensi...]
    all_to_all x1 -> x0, blocking collectives: 189 us -> none  [body(): lax.all_to_all(outgoing, 'expert', split_axis=0, concat_axis=1, tiled=True)]
    gather x13 -> x0, local copies, waits for them, and re-layouts: 150 us -> none  [the longest x5 25.6 us: body(): jnp.take_along_axis(logits, routes, axis=1)]
    all_gather x0 -> x2, waiting for transfers between devices: none -> 107 us  [the longest x1 64.1 us: body(): rows_all = lax.all_gather(second_in, 'expert', axis=0, tiled=True)]
    unnamed x135 -> x153, local copies, waits for them, and re-layouts: 9.21 us -> 114 us
    unnamed x8 -> x10, waiting for transfers between devices: 107 us -> 166 us
    all_to_all x4 -> x0, local copies, waits for them, and re-layouts: 35.5 us -> none  [the longest x1 9.77 us: body(): lax.all_to_all(result, 'expert', split_axis=1, concat_axis=0, tiled=True)]
  transfers between devices with their start and end apart: 9 -> 8, of which waited for: 6 -> 6; matrix products, arithmetic and copies ran while one was open for 14% -> 33% of each run, Pallas kernels for 0% -> 0%
where the time goes in v1:
time: 713 us; the launch traced here: 702 us
  waiting for transfers between devices  310 us (43%)
  matrix products  144 us (20%)
  local copies, waits for them, and re-layouts  136 us (19%)
  other arithmetic  69.1 us (10%)
  blocking collectives  24.1 us (3%)
  between operations  15.3 us (2%)
    unnamed x10, waiting for transfers between devices  166 us
    unnamed x153, local copies, waits for them, and re-layouts  114 us
    all_gather x1, waiting for transfers between devices, body(): rows_all = lax.all_gather(second_in, 'expert', axis=0, tiled=True)  64.1 us
    all_gather x1, waiting for transfers between devices, body(): cots_all = lax.all_gather(cotangent, 'expert', axis=0, tiled=True)  42.6 us
    reduce_scatter x1, waiting for transfers between devices, body(): lax.psum_scatter(mix_part.astype(jnp.bfloat16), 'expert', scatter_dimensi...  31.7 us
    all_gather x1, blocking collectives, body(): gates_all = lax.all_gather(gates, 'expert', axis=0, tiled=True)  24.1 us
    dot_general x1, matrix products, body(): jnp.einsum('td,edf->etf', rows_all, expert_in, preferred_element_type=jnp...  21.2 us
    another operation x3, other arithmetic  20.6 us
  transfers between devices with their start and end apart: 8, of which 6 were waited for; matrix products, arithmetic and copies ran while one was open for 33% of the time, Pallas kernels for 0%

profile of v1, /device:TPU:0, one launch (start us, length us, event | category | flops | bytes accessed | tf_op | source)
XLA Modules:
  0.0 702.4 jit_solution(13573894373451961974)
XLA Ops:
  9.5 4.3 fusion.46
  20.4 3.1 copy.265
  23.5 1.6 slice_negate_fusion.1
  27.5 1.9 exponential_reduce_fusion
  29.4 1.7 copy-done.1
  31.1 2.4 convolution_convert_fusion.3
  39.2 64.1 %all-gather.3.cloned.1.call-done = bf16[1536,1024]{1,0:T(8,128)(2,1)} async-done(((bf16[384,1024]{1,0:T(8,128)(2,1)}), bf16[1536,1024]{1,0:T(8,128)(2,1)}) %all-gather.3.cloned.1.call-update) | async-done | bytes 3145744 | tf_op jit(solution)/shard_map/all_gather | solution.py:152
  103.3 21.2 %convolution_bitcast_fusion = f32[4,1536,1024]{1,2,0:T(8,128)} fusion(bf16[4,1024,1024]{2,1,0:T(8,128)(2,1)} %param.46, bf16[1536,1024]{1,0:T(8,128)(2,1)} %all-gather.3.cloned.1.call-done), kind=kOutput, calls=%fused_computation | convolution fusion | flops 12884901888 | bytes 36700160 | tf_op jit(solution)/shard_map/td,edf->etf/dot_general | solution.py:157
  124.5 42.6 %all-gather.5.cloned.1.call-done = bf16[1536,1024]{1,0:T(8,128)(2,1)} async-done(((bf16[384,1024]{1,0:T(8,128)(2,1)}), bf16[1536,1024]{1,0:T(8,128)(2,1)}) %all-gather.5.cloned.1.call-update) | async-done | bytes 3145744 | tf_op jit(solution)/shard_map/all_gather | solution.py:153
  167.0 18.8 %fusion = (f32[4,1536]{1,0:T(4,128)}, f32[4,512,1536]{2,1,0:T(8,128)}) fusion(f32[4,1536,1024]{1,2,0:T(8,128)} %convolution_bitcast_fusion, bf16[4,1024,512]{2,1,0:T(8,128)(2,1)} %param.50, bf16[1536,1024]{1,0:T(8,128)(2,1)} %all-gather.5.cloned.1.call-done), kind=kOutput, calls=%fused_computation.4 | convolution fusion | flops 6464464896 | bytes 45113344 | tf_op jit(solution)/shard_map/td,edf->etf/dot_general | solution.py:165
  185.8 3.3 all-to-all-start
  189.1 5.5 all-to-all-done
  194.7 24.1 %all_gather.10 = f32[1536,16]{0,1:T(8,128)S(1)} all-gather(f32[384,16]{0,1:T(8,128)S(1)} %get-tuple-element.161), channel_id=1, replica_groups=mesh['dp'=8,'expert'=4] {'expert'}, dimensions={0}, use_global_device_ids=true | all-gather | bytes 122880 | tf_op jit(solution)/shard_map/all_gather | solution.py:154
  218.9 20.3 %multiply_convert_fusion.1 = (bf16[4,1536,512]{1,2,0:T(8,128)(2,1)S(1)}, bf16[4,1536,512]{1,2,0:T(8,128)(2,1)}, bf16[4,1536,512]{1,2,0:T(8,128)(2,1)}) fusion(f32[4,512,1536]{2,1,0:T(8,128)} %get-tuple-element.188, f32[4,1536,1024]{1,2,0:T(8,128)} %convolution_bitcast_fusion, f32[4,1536]{1,0:T(4,128)S(1)} %dynamic-slice_bitcast_fusion), kind=kLoop, calls=%fused_computation.6 | loop fusion | flops 53477376 | bytes 56647680 | tf_op jit(solution)/shard_map/convert.13
  239.1 2.7 copy-done.10
  241.8 18.9 %bitcast_convert_fusion = bf16[1536,1024]{1,0:T(8,128)(2,1)} fusion(bf16[4,1024,1024]{2,1,0:T(8,128)(2,1)} %param.46, bf16[4,1536,512]{1,2,0:T(8,128)(2,1)} %get-tuple-element.163, bf16[4,1536,512]{1,2,0:T(8,128)(2,1)S(1)} %get-tuple-element.162), kind=kOutput, calls=%fused_computation.23 | convolution fusion | flops 12911640576 | bytes 24117248 | tf_op jit(solution)/shard_map/etf,edf->td/dot_general | solution.py:173
  260.8 11.3 %bitcast_convert_fusion.1 = bf16[1536,1024]{1,0:T(8,128)(2,1)} fusion(bf16[4,1536,512]{1,2,0:T(8,128)(2,1)} %get-tuple-element.164, bf16[4,1024,512]{2,1,0:T(8,128)(2,1)} %param.50), kind=kOutput, calls=%fused_computation.24 | convolution fusion | flops 6444023808 | bytes 13631488 | tf_op jit(solution)/shard_map/etf,edf->td/dot_general | solution.py:164
  272.1 11.1 %convert_bitcast_fusion.1 = bf16[4,1024,512]{1,2,0:T(8,128)(2,1)} fusion(bf16[4,1536,512]{1,2,0:T(8,128)(2,1)} %get-tuple-element.164, bf16[1536,1024]{1,0:T(8,128)(2,1)} %all-gather.5.cloned.1.call-done), kind=kOutput, calls=%fused_computation.26 | convolution fusion | flops 6444548096 | bytes 13631488 | tf_op jit(solution)/shard_map/td,etf->edf/dot_general | solution.py:180
  283.2 7.9 %copy.322 = bf16[4,1024,512]{2,0,1:T(4,128)(2,1)} copy(bf16[4,1024,512]{1,2,0:T(8,128)(2,1)} %convert_bitcast_fusion.1) | data formatting | bytes 8388608
  291.1 5.7 copy.325
  296.9 19.7 %convert_bitcast_fusion = bf16[4,1024,1024]{1,2,0:T(8,128)(2,1)} fusion(bf16[4,1536,512]{1,2,0:T(8,128)(2,1)} %get-tuple-element.163, bf16[4,1536,512]{1,2,0:T(8,128)(2,1)} %copy-done.10, bf16[1536,1024]{1,0:T(8,128)(2,1)} %all-gather.3.cloned.1.call-done), kind=kOutput, calls=%fused_computation.19 | convolution fusion | flops 12914262016 | bytes 24117248 | tf_op jit(solution)/shard_map/td,etf->edf/dot_general | solution.py:181
  316.6 15.1 %copy.320 = bf16[4,1024,1024]{2,0,1:T(4,128)(2,1)} copy(bf16[4,1024,1024]{1,2,0:T(8,128)(2,1)} %convert_bitcast_fusion) | data formatting | bytes 16777216
  331.6 12.2 %copy.324 = bf16[128,8,4,1024]{3,1,2,0:T(8,128)(2,1)} copy(bf16[128,8,4,1024]{3,2,1,0:T(4,128)(2,1)} %bitcast.159) | data formatting | bytes 16777216
  346.3 3.9 multiply_reduce_fusion
  350.3 31.7 %reduce-scatter.12.cloned.1.call-done = bf16[384,1024]{1,0:T(8,128)(2,1)} async-done(((bf16[1536,1024]{1,0:T(8,128)(2,1)}), bf16[384,1024]{1,0:T(8,128)(2,1)}) %reduce-scatter.12.cloned.1.call-update) | async-done | bytes 786448 | tf_op jit(solution)/shard_map/reduce_scatter | solution.py:177
  381.9 3.5 multiply_add_fusion.1
  386.5 1.9 convolution_convert_fusion.2
  389.9 8.0 %fusion.2 = (f32[8,2,384]{2,1,0:T(2,128)S(1)}, f32[8,384,384,2]{2,1,3,0:T(8,128)}) fusion(f32[8,384,384,2]{2,1,3,0:T(8,128)} %copy-done.1, f32[8,2,384]{2,1,0:T(2,128)S(1)} %bitcast.179, pred[384,384]{0,1:T(8,128)(4,1)S(1)} %copy-done.15, bf16[384,8,64,1]{0,2,3,1:T(8,128)(2,1)S(1)} %bitcast.173, bf16[384,8,2,64]{0,3,2,1:T(8,128)(2,1)S(1)} %bitcast.167), kind=kOutput, calls=%fused_computation.13 | convolution fusion | flops 313780224 | bytes 20250624 | tf_op jit(solution)/shard_map/qkgd,pkd->kgqp/dot_general | solution.py:208
  397.9 11.3 %fusion.4 = bf16[8,2,384,384]{2,3,1,0:T(8,128)(2,1)} fusion(f32[8,384,384,2]{2,1,3,0:T(8,128)} %get-tuple-element.193, f32[8,384,384,2]{2,1,3,0:T(8,128)} %copy-done.1, f32[8,2,384]{2,1,0:T(2,128)S(1)} %get-tuple-element.192, f32[8,2,384]{2,1,0:T(2,128)S(1)} %bitcast.180, pred[384,384]{0,1:T(8,128)(4,1)S(1)} %copy-done.15), kind=kLoop, calls=%fused_computation.15 | loop fusion | flops 14155776 | bytes 23789568 | tf_op jit(solution)/shard_map/convert_element_type | solution.py:212
  409.3 3.4 convolution_multiply_fusion
  417.2 2.4 fusion.34
  419.7 3.3 fusion.28
  423.4 2.6 convolution_convert_fusion.1
  426.1 4.9 convolution_convert_fusion
  430.9 10.8 %concatenate.64 = bf16[1024,3090]{1,0:T(8,128)(2,1)} concatenate(bf16[1024,2048]{1,0:T(8,128)(2,1)} %convolution_convert_fusion, bf16[1024,1024]{1,0:T(8,128)(2,1)} %convolution_convert_fusion.1, bf16[1024,16]{1,0:T(8,128)(2,1)S(1)} %copy-done.26, bf16[1024,1]{1,0:T(8,128)(2,1)S(1)} %broadcast_in_dim.35, bf16[1024,1]{1,0:T(8,128)(2,1)S(1)} %broadcast_in_dim.36), dimensions={1} | concatenate | bytes 12656640 | tf_op jit(solution)/shard_map/concatenate | solution.py:245
  443.1 2.3 copy.282
  445.4 2.3 copy.281
  450.7 3.2 copy.289
  453.9 3.3 copy.288
  457.2 2.9 copy.287
  460.1 2.5 copy.292
  462.6 2.5 copy.291
  465.2 2.6 copy.290
  467.8 2.3 reshape.277
  470.1 2.2 copy.323
  472.3 4.0 multiply_add_fusion.2
  476.3 2.5 copy.302
  478.8 2.5 copy.303
  481.3 2.5 copy.304
  483.9 3.7 fusion.27
  487.6 23.9 %reduce-scatter.18.cloned.1.call-done = bf16[128,4096]{1,0:T(8,128)(2,1)} async-done(((bf16[1024,4096]{1,0:T(8,128)(2,1)}), bf16[128,4096]{1,0:T(8,128)(2,1)}) %reduce-scatter.18.cloned.1.call-update) | async-done | bytes 1048592
  511.5 2.7 reshape.275
  514.2 2.6 copy.321
  516.8 6.4 multiply_add_fusion
  523.3 2.9 copy.299
  526.1 2.9 copy.300
  529.0 2.9 copy.301
  531.9 141.5 %reduce-scatter.16.cloned.1.call-done = bf16[32,3090]{1,0:T(8,128)(2,1)} async-done(((bf16[1024,3090]{1,0:T(8,128)(2,1)}), bf16[32,3090]{1,0:T(8,128)(2,1)}) %reduce-scatter.16.cloned.1.call-update) | async-done | bytes 197776
  673.4 2.1 copy.319
  676.8 4.1 multiply_add_fusion.3
  680.8 2.3 copy.293
  683.2 2.2 copy.294
  686.4 2.5 multiply_add_fusion.5
  689.0 1.9 copy.296
  (194 shorter events, 37.6 us)
Async XLA Ops:
  7.2 26.3 %copy-start = (bf16[1024,1024]{1,0:T(8,128)(2,1)S(1)}, bf16[1024,1024]{1,0:T(8,128)(2,1)}, u32[]{:S(2)}) copy-start(bf16[1024,1024]{1,0:T(8,128)(2,1)} %param.38) | copy-start | bytes 6291460
  7.2 96.1 %all-gather.3.cloned.1.call-start = ((), (), s32[]{:S(2)}) async-start(), calls=%async_computation.6 | async-start | bytes 3932160 | tf_op jit(solution)/shard_map/all_gather | solution.py:152
  8.1 5.7 copy-start.43
  8.1 26.6 %copy-start.39 = (f32[1024,1]{0,1:T(1,128)}, f32[1024,1]{0,1:T(1,128)S(1)}, u32[]{:S(2)}) copy-start(f32[1024,1]{0,1:T(1,128)S(1)} %get-tuple-element.181) | copy-start | bytes 12292
  9.5 4.3 copy-start.46
  13.9 3.2 copy-start.53
  20.4 5.1 copy-start.19
  20.4 5.1 copy-start.21
  23.5 1.8 copy-start.23
  23.5 2.0 copy-start.2
  25.3 4.1 copy-start.14
  25.5 1.9 copy-start.11
  25.8 1.6 copy-start.7
  27.4 3.7 copy-start.1
  27.5 3.7 copy-start.24
  29.4 4.1 copy-start.32
  31.1 2.4 copy-start.17
  33.5 1.2 copy-start.27
  34.7 1.1 copy-start.3
  34.7 3.0 copy-start.45
  34.7 3.0 copy-start.34
  34.7 2.5 copy-start.41
  36.9 130.1 %all-gather.5.cloned.1.call-start = ((), (), s32[]{:S(2)}) async-start(), calls=%async_computation.8 | async-start | bytes 3932160 | tf_op jit(solution)/shard_map/all_gather | solution.py:153
  185.8 8.9 %all-to-all-start = ((f32[4,384,4]{1,2,0:T(4,128)}), f32[4,384,4]{1,2,0:T(4,128)S(1)}, u32[]{:S(2)}, u32[]{:S(2)}) async-start(f32[4,384,4]{1,2,0:T(4,128)} %bitcast.24), calls=%async_computation.2 | async-start | bytes 49152 | tf_op jit(solution)/shard_map/all_to_all | solution.py:185
  189.1 157.2 %reduce-scatter.14.cloned.1.call-start = ((), (), s32[]{:S(2)}) async-start(), calls=%async_computation.9 | async-start | bytes 3932160 | tf_op jit(solution)/shard_map/reduce_scatter | solution.py:174
  239.1 2.7 copy-start.10
  260.7 121.2 %reduce-scatter.12.cloned.1.call-start = ((), (), s32[]{:S(2)}) async-start(), calls=%async_computation.7 | async-start | bytes 3932160 | tf_op jit(solution)/shard_map/reduce_scatter | solution.py:177
  272.1 195.7 %reduce-scatter.20.cloned.1.call-start = ((), (), s32[]{:S(2)}) async-start(), calls=%async_computation.12 | async-start | bytes 4718592
  296.8 214.7 %reduce-scatter.18.cloned.1.call-start = ((), (), s32[]{:S(2)}) async-start(), calls=%async_computation.11 | async-start | bytes 9437184
  343.9 2.4 copy-start.35
  343.9 2.4 copy-start.40
  343.9 2.4 copy-start.42
  343.9 329.5 %reduce-scatter.16.cloned.1.call-start = ((), (), s32[]{:S(2)}) async-start(), calls=%async_computation.10 | async-start | bytes 6758400
  345.4 36.5 %copy-start.16 = (bf16[384,1024]{1,0:T(8,128)(2,1)S(1)}, bf16[384,1024]{1,0:T(8,128)(2,1)}, u32[]{:S(2)}) copy-start(bf16[384,1024]{1,0:T(8,128)(2,1)} %param.28) | copy-start | bytes 2359300
  386.5 3.4 copy-start.15
  386.5 3.4 copy-start.25
  386.5 3.4 copy-start.33
  397.9 11.4 %copy-start.12 = (bf16[384,8,64,1]{0,2,3,1:T(8,128)(2,1)S(1)}, bf16[384,8,64,1]{0,2,3,1:T(8,128)(2,1)}, u32[]{:S(2)}) copy-start(bf16[384,8,64,1]{0,2,3,1:T(8,128)(2,1)} %copy-done.11) | copy-start | bytes 1179652
  409.3 3.5 copy-start.20
  409.3 4.9 slice-start.3
  412.7 1.5 slice-start.4
  412.8 3.4 slice-start
  413.1 1.3 copy-start.8
  413.1 1.2 copy-start.29
  413.1 3.7 slice-start.1
  414.3 1.7 copy-start.30
  414.3 2.9 slice-start.2
  417.2 2.4 copy-start.18
  417.2 2.4 copy-start.44
  417.2 2.4 copy-start.47
  417.2 2.4 copy-start.54
  419.7 3.8 copy-start.5
  419.7 3.8 copy-start.28
  426.1 4.9 copy-start.26
  441.8 5.9 copy-start.36
  443.0 5.6 copy-start.37
  443.0 6.6 copy-start.38
  676.8 4.1 copy-start.9
  680.8 4.6 copy-start.13
  686.4 6.1 copy-start.51
  686.4 6.1 copy-start.52
  686.4 7.4 %copy-start.48 = (f32[32,16]{0,1:T(8,128)S(1)}, f32[32,16]{0,1:T(8,128)}, u32[]{:S(2)}) copy-start(f32[32,16]{0,1:T(8,128)} %param.45) | copy-start | bytes 6148
  686.4 7.4 %copy-start.49 = (f32[32,16]{0,1:T(8,128)S(1)}, f32[32,16]{0,1:T(8,128)}, u32[]{:S(2)}) copy-start(f32[32,16]{0,1:T(8,128)} %param.43) | copy-start | bytes 6148
  686.4 7.4 %copy-start.50 = (f32[32,16]{0,1:T(8,128)S(1)}, f32[32,16]{0,1:T(8,128)}, u32[]{:S(2)}) copy-start(f32[32,16]{0,1:T(8,128)} %param.44) | copy-start | bytes 6148
  (4 other events, 4.3 us)
Sparse Core Ops, SparseCore 0:
  37.0 66.1 all-gather.2
  104.8 62.1 all-gather.4
  260.8 58.5 reduce-scatter.13
  321.6 60.2 reduce-scatter.11
  385.1 51.3 reduce-scatter.19
  440.2 71.2 reduce-scatter.17
  513.8 159.5 reduce-scatter.15

commit v2 on v1

--- a/solution.py
+++ b/solution.py
@@ -1,6 +1,10 @@
+import functools
+
 import jax
 import jax.numpy as jnp
 from jax import lax
+from jax.experimental import pallas as pl
+from jax.experimental.pallas import tpu as pltpu
 from jax.sharding import PartitionSpec as P
 
 HEADS = 16
@@ -75,6 +79,364 @@
     moment_next = MOMENTUM * moment + gradient
     master_next = master - RATE * (gradient + MOMENTUM * moment_next)
     return (master_next, moment_next, DECAY * average + (1.0 - DECAY) * master_next)
+
+
+F32 = jnp.float32
+BF16 = jnp.bfloat16
+MESH = pl.DeviceIdType.MESH
+VMEM_MOST = 60 * 2**20
+
+
+def contract(left, right, left_axis, right_axis):
+    return lax.dot_general(
+        left, right, (((left_axis,), (right_axis,)), ((), ())), preferred_element_type=F32
+    )
+
+
+def visit_order(line):
+    return [sorted(range(line), key=lambda s: (abs(s - z), s)) for z in range(line)]
+
+
+def pick(table, row, column):
+    value = jnp.int32(table[0][0])
+    for r in range(len(table)):
+        for c in range(len(table[0])):
+            value = jnp.where((row == r) & (column == c), jnp.int32(table[r][c]), value)
+    return value
+
+
+def bank_kernel(
+    line,
+    rows_hbm,
+    cots_hbm,
+    gates_hbm,
+    up_hbm,
+    down_hbm,
+    mix_hbm,
+    back_hbm,
+    gate_grads_hbm,
+    gated_hbm,
+    inner_hbm,
+    rows_all_hbm,
+    rows,
+    cots,
+    gates,
+    gate_grads,
+    gate_grads_sent,
+    up,
+    down,
+    mix_sum,
+    back_sum,
+    stage,
+    gated,
+    inner,
+    columns,
+    row_send,
+    row_recv,
+    gate_send,
+    gate_recv,
+    weight_sem,
+    local_sem,
+    out_sem,
+    grad_send,
+    grad_recv,
+):
+    dp = lax.axis_index("dp")
+    z = lax.axis_index("expert")
+    experts, width, ff_width = down.shape
+
+    def weight_copies(e):
+        return (
+            pltpu.make_async_copy(up_hbm.at[e], up.at[e], weight_sem.at[0, e]),
+            pltpu.make_async_copy(down_hbm.at[e], down.at[e], weight_sem.at[1, e]),
+        )
+
+    for e in range(experts):
+        for copy in weight_copies(e):
+            copy.start()
+    own_rows = pltpu.make_async_copy(rows_hbm, rows.at[z], local_sem.at[0])
+    own_rows.start()
+    all_cots = pltpu.make_async_copy(cots_hbm, cots, local_sem.at[1])
+    all_cots.start()
+    own_gates = pltpu.make_async_copy(gates_hbm.at[z], gates.at[z], local_sem.at[2])
+    own_gates.start()
+
+    barrier = pltpu.get_barrier_semaphore()
+    for step in range(1, line):
+        pl.semaphore_signal(
+            barrier, inc=1, device_id=(dp, lax.rem(z + step, line)), device_id_type=MESH
+        )
+    pl.semaphore_wait(barrier, line - 1)
+
+    def row_copy(source, block, sem, target):
+        return pltpu.make_async_remote_copy(
+            src_ref=source,
+            dst_ref=rows.at[block],
+            send_sem=row_send.at[sem],
+            recv_sem=row_recv.at[block],
+            device_id=(dp, target),
+            device_id_type=MESH,
+        )
+
+    @pl.when(z < line - 1)
+    def _():
+        row_copy(rows_hbm, z, line, z + 1).start()
+
+    @pl.when(z > 0)
+    def _():
+        row_copy(rows_hbm, z, line + 1, z - 1).start()
+
+    def gate_copy(step):
+        peer = lax.rem(z + step, line)
+        return pltpu.make_async_remote_copy(
+            src_ref=gates_hbm.at[peer],
+            dst_ref=gates.at[z],
+            send_sem=gate_send.at[step],
+            recv_sem=gate_recv.at[step],
+            device_id=(dp, peer),
+            device_id_type=MESH,
+        )
+
+    for step in range(1, line):
+        gate_copy(step).start()
+    own_rows.wait()
+    all_cots.wait()
+    own_gates.wait()
+    for step in range(1, line):
+        gate_copy(step).wait()
+
+    order = visit_order(line)
+
+    def out_copies(slot, block):
+        return (
+            pltpu.make_async_copy(stage.at[slot, 0], mix_hbm.at[block], out_sem.at[slot, 0]),
+            pltpu.make_async_copy(stage.at[slot, 1], back_hbm.at[block], out_sem.at[slot, 1]),
+            pltpu.make_async_copy(gated.at[slot], gated_hbm.at[block], out_sem.at[slot, 2]),
+            pltpu.make_async_copy(inner.at[slot], inner_hbm.at[block], out_sem.at[slot, 3]),
+        )
+
+    def grad_copy(block, step):
+        return pltpu.make_async_remote_copy(
+            src_ref=gate_grads_sent.at[block],
+            dst_ref=gate_grads.at[z],
+            send_sem=grad_send.at[block],
+            recv_sem=grad_recv.at[z],
+            device_id=(dp, block),
+            device_id_type=MESH,
+        )
+
+    def visit(k, _):
+        block = pick(order, z, k)
+        slot = lax.rem(k, 2)
+        apart = jnp.abs(block - z)
+        previous = pick(order, z, jnp.maximum(k - 1, 0))
+        first = (k > 0) & (apart != jnp.abs(previous - z))
+        below = z - apart
+        above = z + apart
+
+        @pl.when(first & (below >= 0))
+        def _():
+            low = jnp.maximum(below, 0)
+            row_copy(rows_hbm, low, low, z).wait_recv()
+
+            @pl.when(z < line - 1)
+            def _():
+                row_copy(rows.at[low], low, low, z + 1).start()
+
+        @pl.when(first & (above < line))
+        def _():
+            high = jnp.minimum(above, line - 1)
+            row_copy(rows_hbm, high, high, z).wait_recv()
+
+            @pl.when(z > 0)
+            def _():
+                row_copy(rows.at[high], high, high, z - 1).start()
+
+        @pl.when(k >= 2)
+        def _():
+            for copy in out_copies(slot, pick(order, z, jnp.maximum(k - 2, 0))):
+                copy.wait()
+
+        mix_sum[...] = jnp.zeros_like(mix_sum)
+        back_sum[...] = jnp.zeros_like(back_sum)
+        columns[...] = jnp.zeros_like(columns)
+        gate_columns = gates[block].T
+        lane = lax.broadcasted_iota(jnp.int32, gate_columns.shape, 1)
+        wide_lane = lax.broadcasted_iota(jnp.int32, columns.shape, 1)
+
+        def expert(e, _):
+            @pl.when(k == 0)
+            def _():
+                for copy in weight_copies(e):
+                    copy.wait()
+
+            gate_col = jnp.sum(jnp.where(lane == e, gate_columns, 0.0), axis=1, keepdims=True)
+            both = contract(rows[block], up[e], 1, 0)
+            returned = contract(cots[block], down[e], 1, 0)
+            gate_part = both[:, :ff_width]
+            up_part = both[:, ff_width:]
+            sigmoid_gate = jax.nn.sigmoid(gate_part)
+            silu_gate = gate_part * sigmoid_gate
+            active = silu_gate * up_part
+            gated_part = (active * gate_col).astype(BF16)
+            gated[slot, :, pl.ds(pl.multiple_of(e * ff_width, ff_width), ff_width)] = gated_part
+            mix_sum[...] += contract(gated_part, down[e], 1, 1)
+            gate_grad = jnp.sum(active * returned, axis=1, keepdims=True)
+            columns[...] = jnp.where(wide_lane == e, gate_grad, columns[...])
+            scaled = returned * gate_col
+            grad_gate = scaled * up_part * (sigmoid_gate * (1.0 + gate_part * (1.0 - sigmoid_gate)))
+            grad_up = scaled * silu_gate
+            grads = jnp.concatenate([grad_gate, grad_up], axis=1).astype(BF16)
+            inner[slot, :, pl.ds(pl.multiple_of(e * 2 * ff_width, ff_width), 2 * ff_width)] = grads
+            back_sum[...] += contract(grads, up[e], 1, 1)
+            return 0
+
+        lax.fori_loop(0, experts, expert, 0)
+        stage[slot, 0] = mix_sum[...].astype(BF16)
+        stage[slot, 1] = back_sum[...].astype(BF16)
+        for copy in out_copies(slot, block):
+            copy.start()
+        gate_grads_sent[block] = columns[...].T[: gate_grads.shape[1]]
+
+        @pl.when(block == z)
+        def _():
+            gate_grads[z] = gate_grads_sent[z]
+
+        @pl.when(block != z)
+        def _():
+            grad_copy(block, 0).start()
+
+        return 0
+
+    lax.fori_loop(0, line, visit, 0)
+    for k in (line - 2, line - 1):
+        for copy in out_copies(k % 2, pick(order, z, k)):
+            copy.wait()
+
+    @pl.when(z < line - 1)
+    def _():
+        row_copy(rows_hbm, z, line, z + 1).wait_send()
+
+    @pl.when(z > 0)
+    def _():
+        row_copy(rows_hbm, z, line + 1, z - 1).wait_send()
+
+    for s in range(line):
+
+        @pl.when(((s < z) & (z < line - 1)) | ((s > z) & (z > 0)))
+        def _(s=s):
+            row_copy(rows_hbm, s, s, z).wait_send()
+
+        @pl.when(s != z)
+        def _(s=s):
+            grad_copy(s, 0).wait_send()
+            pltpu.make_async_remote_copy(
+                src_ref=gate_grads_sent.at[s],
+                dst_ref=gate_grads.at[s],
+                send_sem=grad_send.at[s],
+                recv_sem=grad_recv.at[s],
+                device_id=(dp, z),
+                device_id_type=MESH,
+            ).wait_recv()
+
+    last = (
+        pltpu.make_async_copy(rows, rows_all_hbm, local_sem.at[0]),
+        pltpu.make_async_copy(gate_grads, gate_grads_hbm, local_sem.at[1]),
+    )
+    for copy in last:
+        copy.start()
+    for copy in last:
+        copy.wait()
+
+
+def bank(rows, cots, gates, up, down, line):
+    tokens, width = rows.shape
+    experts, _, ff_width = down.shape
+    shape = jax.ShapeDtypeStruct
+    held = gates.shape[1:]
+    anywhere = pl.BlockSpec(memory_space=pl.ANY)
+    work = 10 * line * tokens * experts * width * ff_width
+    return pl.pallas_call(
+        functools.partial(bank_kernel, line),
+        out_shape=(
+            shape((line, tokens, width), BF16),
+            shape((line, tokens, width), BF16),
+            shape((line,) + held, F32),
+            shape((line, tokens, experts * ff_width), BF16),
+            shape((line, tokens, experts * 2 * ff_width), BF16),
+            shape((line, tokens, width), BF16),
+        ),
+        in_specs=[anywhere] * 5,
+        out_specs=(anywhere,) * 6,
+        scratch_shapes=[
+            pltpu.VMEM((line, tokens, width), BF16),
+            pltpu.VMEM((line, tokens, width), BF16),
+            pltpu.VMEM((line,) + held, F32),
+            pltpu.VMEM((line,) + held, F32),
+            pltpu.VMEM((line,) + held, F32),
+            pltpu.VMEM(up.shape, BF16),
+            pltpu.VMEM(down.shape, BF16),
+            pltpu.VMEM((tokens, width), F32),
+            pltpu.VMEM((tokens, width), F32),
+            pltpu.VMEM((2, 2, tokens, width), BF16),
+            pltpu.VMEM((2, tokens, experts * ff_width), BF16),
+            pltpu.VMEM((2, tokens, experts * 2 * ff_width), BF16),
+            pltpu.VMEM((tokens, 128), F32),
+            pltpu.SemaphoreType.DMA((line + 2,)),
+            pltpu.SemaphoreType.DMA((line,)),
+            pltpu.SemaphoreType.DMA((line,)),
+            pltpu.SemaphoreType.DMA((line,)),
+            pltpu.SemaphoreType.DMA((2, experts)),
+            pltpu.SemaphoreType.DMA((3,)),
+            pltpu.SemaphoreType.DMA((2, 4)),
+            pltpu.SemaphoreType.DMA((line,)),
+            pltpu.SemaphoreType.DMA((line,)),
+        ],
+        compiler_params=pltpu.CompilerParams(
+            collective_id=1, has_side_effects=True, vmem_limit_bytes=VMEM_MOST
+        ),
+        cost_estimate=pl.CostEstimate(flops=work, bytes_accessed=2**26, transcendentals=0),
+    )(rows, cots, gates, up, down)
+
+
+def weight_grads_kernel(rows, cots, gated, inner, up_grad, down_grad):
+    step = 256
+    for at in range(0, rows.shape[1], step):
+        up_grad[0, at : at + step] = contract(rows[:, at : at + step], inner[...], 0, 0).astype(BF16)
+        down_grad[0, at : at + step] = contract(cots[:, at : at + step], gated[...], 0, 0).astype(
+            BF16
+        )
+
+
+def weight_grads(rows, cots, gated, inner, experts):
+    tokens, width = rows.shape
+    ff_width = gated.shape[1] // experts
+    whole = pl.BlockSpec((tokens, width), lambda e: (0, 0))
+    return pl.pallas_call(
+        weight_grads_kernel,
+        grid=(experts,),
+        out_shape=(
+            jax.ShapeDtypeStruct((experts, width, 2 * ff_width), BF16),
+            jax.ShapeDtypeStruct((experts, width, ff_width), BF16),
+        ),
+        in_specs=[
+            whole,
+            whole,
+            pl.BlockSpec((tokens, ff_width), lambda e: (0, e)),
+            pl.BlockSpec((tokens, 2 * ff_width), lambda e: (0, e)),
+        ],
+        out_specs=(
+            pl.BlockSpec((1, width, 2 * ff_width), lambda e: (e, 0, 0)),
+            pl.BlockSpec((1, width, ff_width), lambda e: (e, 0, 0)),
+        ),
+        compiler_params=pltpu.CompilerParams(vmem_limit_bytes=VMEM_MOST),
+        cost_estimate=pl.CostEstimate(
+            flops=6 * tokens * width * experts * ff_width,
+            bytes_accessed=2 * tokens * (2 * width + 3 * experts * ff_width)
+            + 6 * experts * width * ff_width,
+            transcendentals=0,
+        ),
+    )(rows, cots, gated, inner)
 
 
 def body(
@@ -110,7 +472,6 @@
     local_experts = expert_in.shape[0]
     peer_count = lax.axis_size("expert")
     experts = local_experts * peer_count
-    ff_width = expert_out.shape[2]
     group_size = HEADS // KV_HEADS
     query_end = HEADS * HEAD_DIM
     key_end = query_end + KV_HEADS * HEAD_DIM
@@ -148,47 +509,35 @@
     powers = jnp.where(named, jnp.exp(logits - peak), 0.0)
     gates = powers / jnp.sum(powers, axis=1, keepdims=True)
     incoming = cotangent.astype(jnp.float32)
-    slots = lax.axis_index("expert") * local_experts
-    rows_all = lax.all_gather(second_in, "expert", axis=0, tiled=True)
-    cots_all = lax.all_gather(cotangent, "expert", axis=0, tiled=True)
-    gates_all = lax.all_gather(gates, "expert", axis=0, tiled=True)
-    gates_here = lax.dynamic_slice_in_dim(gates_all, slots, local_experts, 1)
-    gate_col = gates_here.T[:, :, None]
-    gate_up = jnp.einsum("td,edf->etf", rows_all, expert_in, preferred_element_type=jnp.float32)
-    gate_part = gate_up[..., :ff_width]
-    up_part = gate_up[..., ff_width:]
-    sigmoid_gate = jax.nn.sigmoid(gate_part)
-    silu_gate = gate_part * sigmoid_gate
-    active = silu_gate * up_part
-    gated = (active * gate_col).astype(jnp.bfloat16)
-    mix_part = jnp.einsum("etf,edf->td", gated, expert_out, preferred_element_type=jnp.float32)
-    back = jnp.einsum("td,edf->etf", cots_all, expert_out, preferred_element_type=jnp.float32)
-    gate_grads_here = jnp.sum(active * back, axis=-1).T
-    grad_activated = back * gate_col
-    grad_gate_part = (
-        grad_activated * up_part * sigmoid_gate * (1.0 + gate_part * (1.0 - sigmoid_gate))
-    )
-    grad_up_part = grad_activated * silu_gate
-    grad_gate_up = jnp.concatenate([grad_gate_part, grad_up_part], axis=-1).astype(jnp.bfloat16)
-    grad_part = jnp.einsum("etf,edf->td", grad_gate_up, expert_in, preferred_element_type=jnp.float32)
+    cots_all = lax.all_gather(cotangent, "expert", axis=0, tiled=False)
+    padded = -local_experts % 8
+    gate_rows = jnp.pad(
+        gates.T.reshape(peer_count, local_experts, token_count), ((0, 0), (0, padded), (0, 0))
+    )
+    mix_part, grad_part, gate_grads, gated, grad_gate_up, rows_all = bank(
+        second_in, cots_all, gate_rows, expert_in, expert_out, peer_count
+    )
     grad_second = lax.psum_scatter(
-        grad_part.astype(jnp.bfloat16), "expert", scatter_dimension=0, tiled=True
+        grad_part.reshape(peer_count * token_count, model_width),
+        "expert",
+        scatter_dimension=0,
+        tiled=True,
     ).astype(jnp.float32)
     mixture = lax.psum_scatter(
-        mix_part.astype(jnp.bfloat16), "expert", scatter_dimension=0, tiled=True
+        mix_part.reshape(peer_count * token_count, model_width),
+        "expert",
+        scatter_dimension=0,
+        tiled=True,
     ).astype(jnp.float32)
-    grad_expert_out = jnp.einsum("td,etf->edf", cots_all, gated, preferred_element_type=jnp.float32)
-    grad_expert_in = jnp.einsum(
-        "td,etf->edf", rows_all, grad_gate_up, preferred_element_type=jnp.float32
+    grad_expert_in, grad_expert_out = weight_grads(
+        rows_all.reshape(peer_count * token_count, model_width),
+        cots_all.reshape(peer_count * token_count, model_width),
+        gated.reshape(peer_count * token_count, -1),
+        grad_gate_up.reshape(peer_count * token_count, -1),
+        local_experts,
     )
     output = (hidden + mixture).astype(jnp.bfloat16)
-    grad_gates = lax.all_to_all(
-        gate_grads_here.reshape(peer_count, token_count, local_experts),
-        "expert",
-        split_axis=0,
-        concat_axis=0,
-    )
-    grad_gates = jnp.transpose(grad_gates, (1, 0, 2)).reshape(token_count, experts)
+    grad_gates = gate_grads[:, :local_experts].reshape(experts, token_count).T
     grad_logits = gates * (grad_gates - jnp.sum(gates * grad_gates, axis=1, keepdims=True))
     grad_router = jnp.dot(second_in.astype(jnp.float32).T, grad_logits, precision=HIGHEST)
     grad_second = grad_second + jnp.dot(

time: 713 us -> 621 us (0.87)
  Pallas kernels: 0 us -> 119 us
  matrix products: 144 us -> 48.4 us
  local copies, waits for them, and re-layouts: 136 us -> 60.8 us
  blocking collectives: 24.1 us -> 0 us
  other arithmetic: 69.1 us -> 47.7 us
  waiting for transfers between devices: 310 us -> 319 us
    pallas_call x0 -> x2, Pallas kernels: none -> 119 us  [the longest x1 93.2 us: bank(): pl.pallas_call(functools.partial(bank_kernel, line), out_shape=(shape((li...]
    dot_general x6 -> x0, matrix products: 101 us -> none  [the longest x1 21.2 us: body(): jnp.einsum('td,edf->etf', rows_all, expert_in, preferred_element_type=jnp...]
    reduce_scatter x2 -> x4, waiting for transfers between devices: 31.7 us -> 129 us  [the longest x1 58 us: body(): lax.psum_scatter(mix_part.reshape(peer_count * token_count, model_width),...]
    unnamed x153 -> x117, local copies, waits for them, and re-layouts: 114 us -> 31.1 us
    all_gather x2 -> x1, waiting for transfers between devices: 107 us -> 33.3 us  [body(): cots_all = lax.all_gather(cotangent, 'expert', axis=0, tiled=False)]
    all_gather x1 -> x0, blocking collectives: 24.1 us -> none  [body(): gates_all = lax.all_gather(gates, 'expert', axis=0, tiled=True)]
    another operation x3 -> x2, other arithmetic: 20.6 us -> 0.33 us
    unnamed x10 -> x7, waiting for transfers between devices: 166 us -> 157 us
  transfers between devices with their start and end apart: 8 -> 6, of which waited for: 6 -> 5; matrix products, arithmetic and copies ran while one was open for 33% -> 20% of each run, Pallas kernels for 0% -> 4%
where the time goes in v2:
time: 621 us; the launch traced here: 611 us
  waiting for transfers between devices  319 us (51%)
  Pallas kernels  119 us (19%)
  local copies, waits for them, and re-layouts  60.8 us (10%)
  matrix products  48.4 us (8%)
  other arithmetic  47.7 us (8%)
  between operations  15.2 us (2%)
    unnamed x7, waiting for transfers between devices  157 us
    pallas_call x1, Pallas kernels, bank(): pl.pallas_call(functools.partial(bank_kernel, line), out_shape=(shape((li...  93.2 us
    reduce_scatter x1, waiting for transfers between devices, body(): lax.psum_scatter(mix_part.reshape(peer_count * token_count, model_width),...  58 us
    reduce_scatter x1, waiting for transfers between devices, body(): lax.psum_scatter(grad_expert_in.astype(jnp.bfloat16), 'dp', scatter_dimen...  46.5 us
    all_gather x1, waiting for transfers between devices, body(): cots_all = lax.all_gather(cotangent, 'expert', axis=0, tiled=False)  33.3 us
    unnamed x117, local copies, waits for them, and re-layouts  31.1 us
    pallas_call x1, Pallas kernels, weight_grads(): pl.pallas_call(weight_grads_kernel, grid=(experts,), out_shape=(jax.Shape...  26 us
    reduce_scatter x1, waiting for transfers between devices, body(): lax.psum_scatter(grad_part.reshape(peer_count * token_count, model_width)...  24.1 us
  transfers between devices with their start and end apart: 6, of which 5 were waited for; matrix products, arithmetic and copies ran while one was open for 20% of the time, Pallas kernels for 4%

profile of v2, /device:TPU:0, one launch (start us, length us, event | category | flops | bytes accessed | tf_op | source)
XLA Modules:
  0.0 610.8 jit_solution(1403929796821208873)
XLA Ops:
  8.0 1.4 fusion.60
  9.4 1.4 fusion.17
  10.8 4.3 fusion.34
  15.2 0.9 slice.84
  16.1 1.2 slice.87
  17.3 0.9 copy.155
  18.5 1.5 copy.156
  21.0 3.2 copy.157
  24.4 1.2 fusion.30
  26.8 1.6 fusion.4
  28.4 1.9 exponential_reduce_fusion
  30.3 1.6 copy-done.1
  31.9 2.4 convolution_convert_fusion.3
  34.3 1.1 multiply_reduce_fusion.2
  35.5 1.1 copy-done.5
  39.8 1.4 reshape.274
  41.2 1.4 pad.5.gates_hbm
  42.6 33.3 %all-gather.3.cloned.1.call-done.cots = bf16[1536,1024]{1,0:T(8,128)(2,1)} async-done(((bf16[384,1024]{1,0:T(8,128)(2,1)}), bf16[1536,1024]{1,0:T(8,128)(2,1)}) %all-gather.3.cloned.1.call-update) | async-done | bytes 3145744 | tf_op jit(solution)/shard_map/all_gather | solution.py:512
  75.8 93.2 %shard_map.410 = (bf16[4,384,1024]{2,1,0:T(8,128)(2,1)}, bf16[4,384,1024]{2,1,0:T(8,128)(2,1)}, f32[4,8,384]{2,1,0:T(8,128)}, bf16[4,384,2048]{2,1,0:T(8,128)(2,...) custom-call(bf16[384,1024]{1,0:T(8,128)(2,1)} %copy-done.6, bf16[4,384,1024]{2,1,0:T(8,128)(2,1)} %bitcast.151, ...), custom_call_target="tpu_custom_call" | custom-call | flops 32212254720 | bytes 67108864 | tf_op jit(solution)/shard_map/pallas_call | solution.py:359
  169.8 26.0 %shard_map.411 = (bf16[4,1024,1024]{2,1,0:T(8,128)(2,1)}, bf16[4,1024,512]{2,1,0:T(8,128)(2,1)}) custom-call(bf16[1536,1024]{1,0:T(8,128)(2,1)} %bitcast.154, bf16[1536,1024]{1,0:T(8,128)(2,1)} %all-gather.3.cloned.1.call-done.cots, bf16[1536,2048]{1,0:T(8,128)(2,1)} %bitcast.153, bf16[1536,4096]{1,0:T(8,128)(2,1)} %bitcast.152), custom_call_target="tpu_custom_call" | custom-call | flops 19327352832 | bytes 37748736 | tf_op jit(solution)/shard_map/pallas_call | solution.py:415
  196.7 1.4 slice.74
  198.1 1.4 reshape.277
  200.8 2.2 convolution_convert_fusion.4
  203.0 1.6 copy.165
  204.6 24.1 %reduce-scatter.10.cloned.1.call-done = bf16[384,1024]{1,0:T(8,128)(2,1)} async-done(((bf16[1536,1024]{1,0:T(8,128)(2,1)}), bf16[384,1024]{1,0:T(8,128)(2,1)}) %reduce-scatter.10.cloned.1.call-update) | async-done | bytes 786448 | tf_op jit(solution)/shard_map/reduce_scatter | solution.py:520
  228.7 4.6 multiply_reduce_fusion
  233.3 58.0 %reduce-scatter.8.cloned.1.call-done = bf16[384,1024]{1,0:T(8,128)(2,1)} async-done(((bf16[1536,1024]{1,0:T(8,128)(2,1)}), bf16[384,1024]{1,0:T(8,128)(2,1)}) %reduce-scatter.8.cloned.1.call-update) | async-done | bytes 786448 | tf_op jit(solution)/shard_map/reduce_scatter | solution.py:526
  291.3 3.7 multiply_add_fusion.1
  295.1 1.1 copy-done.3
  296.2 1.9 convolution_convert_fusion.2
  298.1 2.3 copy.160
  300.4 11.9 %fusion = (f32[8,2,384]{2,1,0:T(2,128)}, f32[8,384,384,2]{2,1,3,0:T(8,128)}) fusion(f32[8,384,384,2]{2,1,3,0:T(8,128)} %copy-done.1, f32[8,2,384]{2,1,0:T(2,128)S(1)} %bitcast.137, pred[384,384]{0,1:T(8,128)(4,1)S(1)} %fusion.29, bf16[384,8,64,1]{0,2,3,1:T(8,128)(2,1)} %bitcast.130, bf16[384,8,2,64]{0,3,2,1:T(8,128)(2,1)} %bitcast.124), kind=kOutput, calls=%fused_computation.2 | convolution fusion | flops 313780224 | bytes 20250624 | tf_op jit(solution)/shard_map/qkgd,pkd->kgqp/dot_general | solution.py:557
  312.3 11.7 %fusion.2 = bf16[8,2,384,384]{2,3,1,0:T(8,128)(2,1)} fusion(f32[8,384,384,2]{2,1,3,0:T(8,128)} %get-tuple-element.182, f32[8,384,384,2]{2,1,3,0:T(8,128)} %copy-done.1, f32[8,2,384]{2,1,0:T(2,128)} %get-tuple-element.181, f32[8,2,384]{2,1,0:T(2,128)S(1)} %bitcast.138, pred[384,384]{0,1:T(8,128)(4,1)S(1)} %fusion.29), kind=kLoop, calls=%fused_computation.4 | loop fusion | flops 14155776 | bytes 23789568 | tf_op jit(solution)/shard_map/convert_element_type | solution.py:561
  324.0 3.5 convolution_multiply_fusion
  328.0 0.9 copy-done.15
  329.1 1.3 copy-done.20
  330.5 1.5 broadcast_multiply_fusion
  332.2 0.9 copy-done.11
  333.1 2.6 fusion.22
  335.8 3.2 fusion.16
  339.5 2.6 convolution_convert_fusion.1
  342.1 4.5 convolution_convert_fusion
  346.7 10.8 %concatenate.59 = bf16[1024,3090]{1,0:T(8,128)(2,1)} concatenate(bf16[1024,2048]{1,0:T(8,128)(2,1)} %convolution_convert_fusion, bf16[1024,1024]{1,0:T(8,128)(2,1)} %convolution_convert_fusion.1, bf16[1024,16]{1,0:T(8,128)(2,1)S(1)} %copy-done.17, bf16[1024,1]{1,0:T(8,128)(2,1)S(1)} %broadcast_in_dim.35, bf16[1024,1]{1,0:T(8,128)(2,1)S(1)} %broadcast_in_dim.62), dimensions={1} | concatenate | bytes 12656640 | tf_op jit(solution)/shard_map/concatenate | solution.py:594
  357.5 1.0 copy-done.22
  358.9 2.4 copy.170
  361.2 2.3 copy.169
  363.6 1.0 copy.174
  364.6 1.0 copy.173
  365.6 1.0 copy.172
  366.6 3.7 fusion.15
  370.3 4.1 multiply_add_fusion.2
  374.4 46.5 %reduce-scatter.12.cloned.1.call-done = bf16[4,128,1024]{2,1,0:T(8,128)(2,1)} async-done(((bf16[4,1024,1024]{2,1,0:T(8,128)(2,1)}), bf16[4,128,1024]{2,1,0:T(8,128)(2,1)}) %reduce-scatter.12.cloned.1.call-update) | async-done | bytes 1048592 | tf_op jit(solution)/shard_map/reduce_scatter | solution.py:616
  420.9 6.9 %multiply_add_fusion = (f32[4,128,1024]{2,1,0:T(8,128)}, f32[4,128,1024]{2,1,0:T(8,128)}, f32[4,128,1024]{2,1,0:T(8,128)}) fusion(f32[4,128,1024]{2,1,0:T(8,128)} %param.49, f32[4,128,1024]{2,1,0:T(8,128)} %param.47, bf16[4,128,1024]{2,1,0:T(8,128)(2,1)} %reduce-scatter.12.cloned.1.call-done, f32[4,128,1024]{2,1,0:T(8,128)} %param.48), kind=kLoop, calls=%fused_computation.22 | loop fusion | flops 5242880 | bytes 13631488 | tf_op jit(solution)/shard_map/add | solution.py:81
  427.9 155.3 %reduce-scatter.16.cloned.1.call-done = bf16[32,3090]{1,0:T(8,128)(2,1)} async-done(((bf16[1024,3090]{1,0:T(8,128)(2,1)}), bf16[32,3090]{1,0:T(8,128)(2,1)}) %reduce-scatter.16.cloned.1.call-update) | async-done | bytes 197776
  583.1 2.1 copy.191
  585.3 1.4 convert_element_type.98
  587.0 2.1 multiply_add_fusion.3
  589.2 2.3 copy.175
  591.5 2.2 copy.176
  593.7 1.0 copy.177
  594.8 2.6 multiply_add_fusion.5
  597.4 1.9 copy.178
  600.9 1.3 multiply_add_fusion.9
  602.3 1.3 multiply_add_fusion.7
  (150 shorter events, 13.3 us)
Async XLA Ops:
  7.2 27.1 %copy-start = (bf16[1024,1024]{1,0:T(8,128)(2,1)S(1)}, bf16[1024,1024]{1,0:T(8,128)(2,1)}, u32[]{:S(2)}) copy-start(bf16[1024,1024]{1,0:T(8,128)(2,1)} %param.38) | copy-start | bytes 6291460
  7.2 68.6 %all-gather.3.cloned.1.call-start = ((), (), s32[]{:S(2)}) async-start(), calls=%async_computation.9 | async-start | bytes 3932160 | tf_op jit(solution)/shard_map/all_gather | solution.py:512
  7.9 220.7 %reduce-scatter.10.cloned.1.call-start = ((), (), s32[]{:S(2)}) async-start(), calls=%async_computation.6 | async-start | bytes 3932160 | tf_op jit(solution)/shard_map/reduce_scatter | solution.py:520
  9.4 5.7 copy-start.34
  10.8 4.3 copy-start.38
  16.1 2.2 copy-start.45
  19.9 4.4 copy-start.36
  24.1 1.5 copy-start.2
  25.6 0.9 copy-start.14
  28.3 3.6 copy-start.1
  28.3 3.6 copy-start.16
  30.3 4.0 copy-start.23
  31.9 2.4 copy-start.12
  34.3 1.2 copy-start.18
  34.3 2.3 copy-start.30
  35.5 1.1 copy-start.5
  35.5 2.2 copy-start.25
  35.5 1.1 copy-start.32
  36.8 0.9 copy-start.6
  38.1 0.6 copy-start.29
  38.6 0.6 copy-start.31
  169.1 122.2 %reduce-scatter.8.cloned.1.call-start = ((), (), s32[]{:S(2)}) async-start(), calls=%async_computation.5 | async-start | bytes 3932160 | tf_op jit(solution)/shard_map/reduce_scatter | solution.py:526
  169.8 200.5 %reduce-scatter.14.cloned.1.call-start = ((), (), s32[]{:S(2)}) async-start(), calls=%async_computation.8 | async-start | bytes 4718592 | tf_op jit(solution)/shard_map/reduce_scatter | solution.py:619
  195.9 225.0 %reduce-scatter.12.cloned.1.call-start = ((), (), s32[]{:S(2)}) async-start(), calls=%async_computation.7 | async-start | bytes 9437184 | tf_op jit(solution)/shard_map/reduce_scatter | solution.py:616
  196.5 386.7 %reduce-scatter.16.cloned.1.call-start = ((), (), s32[]{:S(2)}) async-start(), calls=%async_computation.10 | async-start | bytes 6758400
  200.3 0.5 copy-start.33
  295.1 1.1 copy-start.3
  296.2 4.2 copy-start.24
  324.0 5.1 slice-start.3
  327.5 1.6 slice-start.4
  327.5 4.7 slice-start
  327.8 1.0 copy-start.15
  327.8 4.4 slice-start.1
  328.9 1.6 copy-start.20
  330.4 1.6 copy-start.21
  330.4 1.8 slice-start.2
  332.0 1.1 copy-start.11
  333.1 2.7 copy-start.13
  333.1 2.7 copy-start.35
  333.1 2.7 copy-start.39
  333.1 2.7 copy-start.46
  335.8 3.5 copy-start.37
  335.8 3.7 copy-start.4
  335.8 3.7 copy-start.19
  342.1 4.5 copy-start.17
  357.5 1.0 copy-start.22
  357.5 6.0 copy-start.26
  358.8 5.8 copy-start.27
  358.8 6.8 %copy-start.28 = (f32[32,1024]{1,0:T(8,128)S(1)}, f32[32,1024]{1,0:T(8,128)}, u32[]{:S(2)}) copy-start(f32[32,1024]{1,0:T(8,128)} %param.40) | copy-start | bytes 393220
  585.3 1.5 copy-start.8
  585.3 1.8 copy-start.9
  587.0 2.1 copy-start.7
  589.2 4.6 copy-start.10
  594.8 6.2 %copy-start.43 = (f32[32,2]{0,1:T(2,128)S(1)}, f32[32,2]{0,1:T(2,128)}, u32[]{:S(2)}) copy-start(f32[32,2]{0,1:T(2,128)} %param.33) | copy-start | bytes 772
  594.8 6.2 %copy-start.44 = (f32[32,2]{0,1:T(2,128)S(1)}, f32[32,2]{0,1:T(2,128)}, u32[]{:S(2)}) copy-start(f32[32,2]{0,1:T(2,128)} %param.32) | copy-start | bytes 772
  594.8 7.5 %copy-start.40 = (f32[32,16]{0,1:T(8,128)S(1)}, f32[32,16]{0,1:T(8,128)}, u32[]{:S(2)}) copy-start(f32[32,16]{0,1:T(8,128)} %param.45) | copy-start | bytes 6148
  594.8 7.5 %copy-start.41 = (f32[32,16]{0,1:T(8,128)S(1)}, f32[32,16]{0,1:T(8,128)}, u32[]{:S(2)}) copy-start(f32[32,16]{0,1:T(8,128)} %param.43) | copy-start | bytes 6148
  594.8 7.5 %copy-start.42 = (f32[32,16]{0,1:T(8,128)S(1)}, f32[32,16]{0,1:T(8,128)}, u32[]{:S(2)}) copy-start(f32[32,16]{0,1:T(8,128)} %param.44) | copy-start | bytes 6148
Sparse Core Ops, SparseCore 0:
  9.6 66.1 all-gather.2
  169.2 59.4 reduce-scatter.9
  231.0 60.2 reduce-scatter.7
  294.5 51.3 reduce-scatter.13
  349.6 71.2 reduce-scatter.11
  423.1 160.0 reduce-scatter.15
